TPU v7x, 32 devices: a whole 2x2x4 slice. The times are simulated.
32 devices in a mesh: dom: 8 (over z, y), sub: 4 (over x, core).
Axes of the slice: x: 2, y: 2, z: 4, core: 2. Of those that a mesh axis runs over, the one named last changes fastest.
Arguments:
- modal_state: float32 [56, 9, 4096], P(None, None, ('dom', 'sub')), may hold values from -6 to 6
- star_mats: float32 [3, 9, 9, 4096], P(None, None, None, ('dom', 'sub')), may hold values from -2 to 2
- face_flux: float32 [2, 4, 9, 9, 4096], P(None, None, None, None, ('dom', 'sub')), may hold values from -1.5 to 1.5
- stiffness: float32 [3, 56, 56], replicated, may hold values from -1 to 1
- stiff_vol: float32 [3, 56, 56], replicated, may hold values from -0.5 to 0.5
- face_proj: float32 [4, 56, 21], replicated, may hold values from -0.75 to 0.75
- face_lifting_matrix: float32 [4, 21, 56], replicated, may hold values from -0.625 to 0.625
- orient_maps: float32 [3, 21, 21], replicated, may hold values from -1.25 to 1.25
- neighbours: int32 [4, 4096], P(None, ('dom', 'sub')), may hold values from -1 to 895
- face_orient: int32 [4, 4096], P(None, ('dom', 'sub')), may hold values from 0 to 2
- send_slots: int32 [2, 1024], P(None, ('dom', 'sub')), may hold values from 0 to 511
- fast_count: int32 [32], P(('dom', 'sub')), may hold values from 1 to 64, as said below
Outputs:
- new_state: float32 [56, 9, 4096], P(None, None, ('dom', 'sub'))
Inputs may be any that keep to these rules, and one draw needn't show every extreme that they name: A device's first fast_count elements form its fast cluster. `send_slots`: entry k of a device's row names the own trace that fills its k-th slot.
All inputs are finite; a program needn't handle non-finite values.
Results may differ from a plain program's by a relative error of at most 0.0003.
Values sent between devices are 32-bit elements; how exact they have to be, the bound alone decides.
A program may use at most 64 MiB of HBM per device.

v0:
```python
import functools

import jax
import jax.numpy as jnp
from jax import lax
from jax.experimental import pallas as pl
from jax.experimental.pallas import tpu as pltpu
from jax.sharding import PartitionSpec as P

DEGREE = 5
LANES = 128
F32 = jnp.float32
BF16 = jnp.bfloat16


def up(value, multiple):
    return -(-value // multiple) * multiple


def split(x):
    hi = x.astype(BF16)
    return hi, (x - hi.astype(F32)).astype(BF16)


def stacked(x):
    hi, lo = split(x)
    return jnp.concatenate([hi, lo], axis=0)


def dot(a, b):
    return jnp.dot(a, b, preferred_element_type=F32)


def dot3(w_stack, z_hi, z_lo, rows):
    both = dot(w_stack, z_hi)
    half = w_stack.shape[0] // 2
    return both[:rows] + both[half : half + rows] + dot(w_stack[:half], z_lo)[:rows]


def grow8(x):
    return jnp.concatenate([x, jnp.zeros((8 - x.shape[0], x.shape[1]), F32)], axis=0)


def row_of(ref, *lead_and_row):
    lead, row = lead_and_row[:-1], lead_and_row[-1]
    return ref[(*lead, pl.ds(row, 1), slice(None))]


def kernel(
    sizes,
    state_hbm,
    star_hbm,
    flux_hbm,
    stiff_hbm,
    vol_hbm,
    proj_hbm,
    lift_hbm,
    maps_hbm,
    near_idx_ref,
    orient_ref,
    slots_ref,
    count_ref,
    out_ref,
    star_ref,
    flux_ref,
    stiff_ref,
    vol_ref,
    proj_ref,
    lift_ref,
    maps_ref,
    load_sem,
    cur,
    nxt,
    part,
    slow,
    acc,
    trace,
    near,
    remote,
    pred_w,
    proj_w,
    upd_w,
    hot_local,
    hot_remote,
    hot_send,
    mask,
    send,
    recv,
    send_sem,
    recv_sem,
    forward_sem,
):
    n_dom, n_sub, modes, fields, face_pad, slots = sizes
    width = fields * LANES
    mode_pad = up(modes, 16)
    fold = LANES // slots
    fold_rows = trace.shape[0] // fold
    group = n_sub * slots
    faces = 4
    vol_rows, face_rows = 3 * mode_pad, faces * face_pad
    loads = [
        pltpu.make_async_copy(source, target, load_sem.at[i])
        for i, (source, target) in enumerate(
            [
                (stiff_hbm, stiff_ref),
                (vol_hbm, vol_ref),
                (proj_hbm, proj_ref),
                (lift_hbm, lift_ref),
                (maps_hbm, maps_ref),
                (state_hbm, out_ref),
                (star_hbm, star_ref),
                (flux_hbm, flux_ref),
            ]
        )
    ]
    for load in loads:
        load.start()
    dom, sub = lax.axis_index("dom"), lax.axis_index("sub")
    has_low, has_high = dom > 0, dom < n_dom - 1

    barrier = pltpu.get_barrier_semaphore()

    def greet(d, s):
        pl.semaphore_signal(
            barrier, inc=1, device_id={"dom": d, "sub": s}, device_id_type=pl.DeviceIdType.MESH
        )

    chips = n_sub // 2
    chip, core = sub // 2, lax.rem(sub, 2)
    sibling = 2 * chip + 1 - core

    greet(dom, sibling)
    for k in range(1, chips):
        greet(dom, 2 * lax.rem(chip + k, chips) + core)

    @pl.when(has_low)
    def _():
        for c in range(chips):
            greet(dom - 1, 2 * c + core)

    @pl.when(has_high)
    def _():
        for c in range(chips):
            greet(dom + 1, 2 * c + core)

    @pl.when(jnp.logical_not(has_low))
    def _():
        recv[:, 1] = jnp.zeros((2, *recv.shape[2:]), F32)

    @pl.when(jnp.logical_not(has_high))
    def _():
        recv[:, 2] = jnp.zeros((2, *recv.shape[2:]), F32)

    trace[fields * face_pad :, :] = jnp.zeros(
        (trace.shape[0] - fields * face_pad, trace.shape[1]), F32
    )
    slow[...] = jnp.zeros_like(slow)

    def one_hot(row, rows):
        at = lax.broadcasted_iota(jnp.int32, (rows, LANES), 0)
        return jnp.where(at == row, 1.0, 0.0).astype(BF16)

    own_count = faces * LANES
    def at_columns(rows, columns, test):
        row = lax.broadcasted_iota(jnp.int32, (rows, columns), 0)
        column = lax.broadcasted_iota(jnp.int32, (rows, columns), 1)
        return jnp.where(test(row, column), 1.0, 0.0).astype(BF16)

    tiled = dot(
        stacked(grow8(slots_ref[...].astype(F32))),
        at_columns(slots, LANES, lambda row, column: column % slots == row),
    )
    tiled = (tiled[:8] + tiled[8:]).astype(jnp.int32)
    for i in range(2):
        hot_send[:, i * LANES : (i + 1) * LANES] = one_hot(tiled[i : i + 1, :], own_count)

    for load in loads[:5]:
        load.wait()

    def grow(x, rows):
        return jnp.concatenate([x, jnp.zeros((rows - x.shape[0], x.shape[1]), F32)], axis=0)

    def shifted(rows, columns, shift):
        return at_columns(rows, columns, lambda row, column: column == row + shift)

    def spread(ref):
        value = None
        for d in range(3):
            term = dot(stacked(grow(ref[d], mode_pad)), shifted(modes, vol_rows, d * mode_pad))
            value = term if value is None else value + term
        return value

    face_modes = maps_ref.shape[1]
    pred_w[...] = (-spread(stiff_ref)).astype(BF16)
    def by_face(ref):
        return jnp.concatenate([grow(ref[:, j, :], face_pad) for j in range(faces)], axis=0)

    proj_w[...] = stacked(by_face(proj_ref))
    def prepare_update():
        for j in range(faces):
            row = near_idx_ref[j : j + 1, :]
            hot_local[:, j * LANES : (j + 1) * LANES] = one_hot(row, own_count)
            hot_remote[:, j * LANES : (j + 1) * LANES] = one_hot(row - own_count, 3 * group)
            turn = orient_ref[j : j + 1, :]
            for o in range(3):
                mask[o, j * face_pad : (j + 1) * face_pad, :] = jnp.broadcast_to(
                    jnp.where(turn == o, 1.0, 0.0), (face_pad, LANES)
                )
        upd_w[:, :vol_rows] = spread(vol_ref).astype(BF16)
        same = shifted(mode_pad, modes, 0)
        turn_lift = []
        for value in split(-by_face(lift_ref)):
            turn_lift.append(
                lax.dot_general(same, value, (((1,), (1,)), ((), ())), preferred_element_type=F32)
            )
        turn_lift = jnp.concatenate(turn_lift, axis=0).astype(BF16)
        upd_w[:, vol_rows : vol_rows + face_rows] = turn_lift
        turned = None
        for o in range(3):
            place = at_columns(
                face_modes,
                3 * face_rows,
                lambda row, column: (column // face_rows == o) & (column % face_pad == row),
            )
            both = dot(stacked(grow(maps_ref[o], up(face_pad, 16))), place)
            term = both[:face_pad] + both[up(face_pad, 16) :][:face_pad]
            turned = term if turned is None else turned + term
        turned = jnp.concatenate([turned] * faces, axis=0)
        row = lax.broadcasted_iota(jnp.int32, turned.shape, 0)
        column = lax.broadcasted_iota(jnp.int32, turned.shape, 1)
        turned = jnp.where(column % face_rows // face_pad == row // face_pad, turned, 0.0)
        upd_w[:, vol_rows + face_rows :] = stacked(dot3(turn_lift, *split(turned), mode_pad))

    for load in loads[5:]:
        load.wait()

    def star_rows(src, f):
        high, low = [], []
        for d in range(3):
            for start in range(0, modes, 16):
                count = min(16, modes - start)
                total = None
                for g in range(fields):
                    term = row_of(star_ref, f, g, d) * src[
                        start : start + count, g * LANES : (g + 1) * LANES
                    ]
                    total = term if total is None else total + term
                if count < 16:
                    total = jnp.concatenate([total, jnp.zeros((16 - count, LANES), F32)], axis=0)
                hi, lo = split(total)
                high.append(hi)
                low.append(lo)
        return jnp.concatenate(high, axis=0), jnp.concatenate(low, axis=0)

    def flux_rows(side, src, f):
        blocks = []
        for j in range(faces):
            total = None
            for g in range(fields):
                term = row_of(flux_ref, side, f, g, j) * src[
                    g * face_pad : (g + 1) * face_pad, j * LANES : (j + 1) * LANES
                ]
                total = term if total is None else total + term
            blocks.append(total)
        return split(jnp.concatenate(blocks, axis=0))

    chunks = [tuple(range(f, min(f + 2, fields))) for f in range(0, fields, 2)]

    def add_out(chunk, value):
        for i, f in enumerate(chunk):
            out_ref[f] = out_ref[f] + value[:, i * LANES : (i + 1) * LANES]

    def side_by_side(pairs):
        return (
            jnp.concatenate([p[0] for p in pairs], axis=1),
            jnp.concatenate([p[1] for p in pairs], axis=1),
        )

    def cols(chunk):
        return slice(chunk[0] * LANES, (chunk[-1] + 1) * LANES)

    def out_copy(ex, which, target, region, lane):
        return pltpu.make_async_remote_copy(
            src_ref=send.at[ex, which],
            dst_ref=recv.at[ex, region, sub],
            send_sem=send_sem.at[ex, region, lane],
            recv_sem=recv_sem.at[ex, region, sub],
            device_id=target,
            device_id_type=pl.DeviceIdType.MESH,
        )

    def exchange_copies(ex):
        inner = [out_copy(ex, 0, {"dom": dom, "sub": sibling}, 0, 0)]
        for k in range(1, chips):
            target = {"dom": dom, "sub": 2 * lax.rem(chip + k, chips) + core}
            inner.append(out_copy(ex, 0, target, 0, k))
        lower = [
            out_copy(ex, 1, {"dom": dom - 1, "sub": 2 * c + core}, 2, c) for c in range(chips)
        ]
        upper = [
            out_copy(ex, 1, {"dom": dom + 1, "sub": 2 * c + core}, 1, c) for c in range(chips)
        ]
        return inner, lower, upper

    def arrival(ex, region, s):
        return pltpu.make_async_remote_copy(
            src_ref=send.at[ex, 0],
            dst_ref=recv.at[ex, region, s],
            send_sem=send_sem.at[ex, region, 0],
            recv_sem=recv_sem.at[ex, region, s],
            device_id={"dom": dom, "sub": sub},
            device_id_type=pl.DeviceIdType.MESH,
        )

    def forward(ex, region, s):
        return pltpu.make_async_remote_copy(
            src_ref=recv.at[ex, region, s],
            dst_ref=recv.at[ex, region, s],
            send_sem=forward_sem.at[ex, region, s],
            recv_sem=recv_sem.at[ex, region, s],
            device_id={"dom": dom, "sub": sibling},
            device_id_type=pl.DeviceIdType.MESH,
        )

    def each_region(do, side):
        @pl.when(has_low)
        def _():
            for c in range(chips):
                do(1, 2 * c + side)

        @pl.when(has_high)
        def _():
            for c in range(chips):
                do(2, 2 * c + side)

        for k in range(1, chips):
            do(0, 2 * lax.rem(chip + k, chips) + side)

    is_fast = lax.broadcasted_iota(jnp.int32, (1, LANES), 1) < count_ref[0]

    def stage(ex, carry):
        for f in range(fields):
            at = slice(f * LANES, (f + 1) * LANES)
            start = out_ref[f]
            cur[:, at] = start
            part[:, at] = start
            acc[:, at] = start

        def order(k, weights):
            weight, power = weights
            for chunk in chunks:
                hi, lo = side_by_side([star_rows(cur, f) for f in chunk])
                nxt[:, cols(chunk)] = dot3(pred_w[...], hi, lo, modes)
            weight = weight / (k.astype(F32) + 2.0)
            power = power * 2.0
            value = nxt[...]
            cur[...] = value
            part[...] = part[...] + weight * value
            acc[...] = acc[...] + ((power - 1.0) * weight) * value
            return weight, power

        lax.fori_loop(0, DEGREE, order, (jnp.float32(1.0), jnp.float32(2.0)))
        keep = jnp.logical_or(is_fast, ex == 0)
        for g in range(fields):
            at = slice(g * LANES, (g + 1) * LANES)
            part[:, at] = jnp.where(keep, part[:, at], slow[:, at])
        slow[...] = acc[...]

        for chunk in chunks:
            hi, lo = split(part[:, cols(chunk)])
            value = dot3(proj_w[...], hi, lo, face_rows)
            for i, g in enumerate(chunk):
                for j in range(faces):
                    trace[g * face_pad : (g + 1) * face_pad, j * LANES : (j + 1) * LANES] = value[
                        j * face_pad : (j + 1) * face_pad, i * LANES : (i + 1) * LANES
                    ]

        table = stacked(trace[...])
        rows = trace.shape[0]
        picked = dot(table, hot_send[...])
        picked = picked[:rows] + picked[rows:]
        section = lax.broadcasted_iota(jnp.int32, (fold_rows, LANES), 1) // slots
        for i in range(2):
            lanes = slice(i * LANES, (i + 1) * LANES)
            packed = picked[:fold_rows, lanes]
            for a in range(1, fold):
                packed = jnp.where(
                    section == a, picked[a * fold_rows : (a + 1) * fold_rows, lanes], packed
                )
            send[ex, i] = packed
            if i == 0:
                recv[ex, 0, sub] = packed

        @pl.when(ex == 0)
        def _():
            pl.semaphore_wait(
                barrier, chips * (1 + has_low.astype(jnp.int32) + has_high.astype(jnp.int32))
            )

        inner, lower, upper = exchange_copies(ex)

        @pl.when(has_low)
        def _():
            for copy in lower:
                copy.start()

        @pl.when(has_high)
        def _():
            for copy in upper:
                copy.start()

        for copy in inner:
            copy.start()

        @pl.when(ex == 0)
        def _():
            prepare_update()

        found = dot(table, hot_local[...])
        near[...] = found[:rows] + found[rows:]
        base = vol_rows + face_rows
        for chunk in chunks:
            pairs = []
            for f in chunk:
                vol, own = star_rows(part, f), flux_rows(0, trace, f)
                pairs.append([jnp.concatenate([vol[i], own[i]], axis=0) for i in range(2)])
            hi, lo = side_by_side(pairs)
            add_out(chunk, dot3(upd_w[:, :base], hi, lo, modes))

        def pass_on(region, s):
            arrival(ex, region, s).wait_recv()
            forward(ex, region, s).start()

        each_region(pass_on, core)
        arrival(ex, 0, sibling).wait_recv()
        each_region(lambda region, s: arrival(ex, region, s).wait_recv(), 1 - core)

        for region in range(3):
            for b in range(n_sub // fold):
                blocks = [recv[ex, region, b * fold + i] for i in range(fold)]
                for a in range(fold):
                    value = None
                    for i in range(fold):
                        moved = blocks[i]
                        if i != a:
                            moved = pltpu.roll(moved, ((i - a) * slots) % LANES, 1)
                        value = moved if value is None else jnp.where(section == i, moved, value)
                    first = region * group + b * LANES
                    remote[a * fold_rows : (a + 1) * fold_rows, first : first + LANES] = value
        found = dot(stacked(remote[...]), hot_remote[...])
        near[...] = near[...] + found[:rows] + found[rows:]

        masks = [mask[o].astype(BF16) for o in range(3)]
        for chunk in chunks:
            pairs = []
            for f in chunk:
                hi, lo = flux_rows(1, near, f)
                pairs.append(
                    [
                        jnp.concatenate([value * masks[o] for o in range(3)], axis=0)
                        for value in (hi, lo)
                    ]
                )
            hi, lo = side_by_side(pairs)
            add_out(chunk, dot3(upd_w[:, base:], hi, lo, modes))

        for copy in inner:
            copy.wait_send()

        @pl.when(has_low)
        def _():
            for copy in lower:
                copy.wait_send()

        @pl.when(has_high)
        def _():
            for copy in upper:
                copy.wait_send()

        each_region(lambda region, s: forward(ex, region, s).wait_send(), core)
        return carry

    lax.fori_loop(0, 2, stage, 0)


def local(
    n_dom,
    n_sub,
    modal_state,
    star_mats,
    face_flux,
    stiffness,
    stiff_vol,
    face_proj,
    face_lifting_matrix,
    orient_maps,
    neighbours,
    face_orient,
    send_slots,
    fast_count,
):
    modes, fields, elems = modal_state.shape
    face_modes = orient_maps.shape[1]
    slots = send_slots.shape[1]
    fold = LANES // slots
    face_pad, mode_pad = up(face_modes, 8), up(modes, 16)
    table_rows = up(fields * face_pad, 8 * fold)
    group = n_sub * slots
    width = fields * elems
    upd_cols = 3 * mode_pad + 4 * 4 * face_pad
    any_space = pl.BlockSpec(memory_space=pl.ANY)
    vmem = pl.BlockSpec(memory_space=pltpu.VMEM)
    out = pl.pallas_call(
        functools.partial(kernel, (n_dom, n_sub, modes, fields, face_pad, slots)),
        out_shape=jax.ShapeDtypeStruct((fields, modes, elems), F32),
        in_specs=[any_space] * 8 + [vmem] * 3 + [pl.BlockSpec(memory_space=pltpu.SMEM)],
        out_specs=vmem,
        scratch_shapes=[
            pltpu.VMEM((fields, fields, 3, elems), F32),
            pltpu.VMEM((2, fields, fields, 4, elems), F32),
            pltpu.VMEM((3, modes, modes), F32),
            pltpu.VMEM((3, modes, modes), F32),
            pltpu.VMEM((face_modes, 4, modes), F32),
            pltpu.VMEM((face_modes, 4, modes), F32),
            pltpu.VMEM((3, face_modes, face_modes), F32),
            pltpu.SemaphoreType.DMA((8,)),
            pltpu.VMEM((modes, width), F32),
            pltpu.VMEM((modes, width), F32),
            pltpu.VMEM((modes, width), F32),
            pltpu.VMEM((modes, width), F32),
            pltpu.VMEM((modes, width), F32),
            pltpu.VMEM((table_rows, 4 * elems), F32),
            pltpu.VMEM((table_rows, 4 * elems), F32),
            pltpu.VMEM((table_rows, 3 * group), F32),
            pltpu.VMEM((2 * mode_pad, 3 * mode_pad), BF16),
            pltpu.VMEM((8 * face_pad, modes), BF16),
            pltpu.VMEM((2 * mode_pad, upd_cols), BF16),
            pltpu.VMEM((4 * elems, 4 * elems), BF16),
            pltpu.VMEM((3 * group, 4 * elems), BF16),
            pltpu.VMEM((4 * elems, 2 * LANES), BF16),
            pltpu.VMEM((3, 4 * face_pad, LANES), F32),
            pltpu.VMEM((2, 2, table_rows // fold, LANES), F32),
            pltpu.VMEM((2, 3, n_sub, table_rows // fold, LANES), F32),
            pltpu.SemaphoreType.DMA((2, 3, n_sub)),
            pltpu.SemaphoreType.DMA((2, 3, n_sub)),
            pltpu.SemaphoreType.DMA((2, 3, n_sub)),
        ],
        compiler_params=pltpu.CompilerParams(collective_id=0, has_side_effects=True),
    )(
        modal_state.transpose(1, 0, 2),
        star_mats.transpose(1, 2, 0, 3),
        face_flux.transpose(0, 2, 3, 1, 4),
        stiffness,
        stiff_vol,
        face_proj.transpose(2, 0, 1),
        face_lifting_matrix.transpose(1, 0, 2),
        orient_maps,
        neighbours,
        face_orient,
        send_slots,
        fast_count,
    )
    return out.transpose(1, 0, 2)


def solution(mesh):
    split_last = ("dom", "sub")
    placed = (
        P(None, None, split_last),
        P(None, None, None, split_last),
        P(None, None, None, None, split_last),
        P(),
        P(),
        P(),
        P(),
        P(),
        P(None, split_last),
        P(None, split_last),
        P(None, split_last),
        P(split_last),
    )
    return jax.shard_map(
        functools.partial(local, mesh.shape["dom"], mesh.shape["sub"]),
        mesh=mesh,
        in_specs=placed,
        out_specs=P(None, None, split_last),
        check_vma=False,
    )
```

profile of v0, /device:TPU:21, one launch (start us, length us, event | category | flops | bytes accessed | tf_op | source)
XLA Modules:
  0.0 28.5 jit_solution(9757209801287945363)
XLA Ops:
  0.7 26.2 %shard_map.118 = f32[9,56,128]{2,1,0:T(8,128)} custom-call(f32[9,56,128]{2,1,0:T(8,128)} %bitcast.8, f32[9,9,3,128]{3,2,1,0:T(4,128)} %bitcast.9, f32[2,9,9,4,128]{4,3,2,1,0:T(4,128)} %bitcast.7, f32[3,56,56]{2,1,0:T(8,128)} %stiff_hbm.1, f32[3,56,56]{2,1,0:T(8,128)} %vol_hbm.1, f32[21,4,56]{2,1,0:T(4,128)} %bitcast.10, f32[21,4,56]{2,1,0:T(4,128)} %bitcast.11, ...), custom_call_target="tpu_custom_call" | custom-call | tf_op jit(solution)/shard_map/pallas_call | solution.py:513
  26.8 1.7 %copy.15 = f32[56,9,128]{2,0,1:T(8,128)} copy(f32[56,9,128]{2,0,1:T(8,128)} %bitcast.6) | data formatting | bytes 516096
where the time goes:
time: 28.7 us; the launch traced here: 28.5 us
  Pallas kernels  26.2 us (91%)
  local copies, waits for them, and re-layouts  1.66 us (6%)
  between operations  0.66 us (2%)
    pallas_call x1, Pallas kernels, local(): pl.pallas_call(functools.partial(kernel, (n_dom, n_sub, modes, fields, fa...  26.2 us
    unnamed x1, local copies, waits for them, and re-layouts  1.66 us

commit v1 on v0

v1 whole, which is shorter than its diff:
```python
import functools

import jax
import jax.numpy as jnp
from jax import lax
from jax.experimental import pallas as pl
from jax.experimental.pallas import tpu as pltpu
from jax.sharding import PartitionSpec as P

DEGREE = 5
LANES = 128
F32 = jnp.float32
BF16 = jnp.bfloat16


def up(value, multiple):
    return -(-value // multiple) * multiple


def split(x):
    hi = x.astype(BF16)
    return hi, (x - hi.astype(F32)).astype(BF16)


def stacked(x):
    hi, lo = split(x)
    return jnp.concatenate([hi, lo], axis=0)


def dot(a, b):
    return jnp.dot(a, b, preferred_element_type=F32)


def rows3(x, depth):
    low = x - x.astype(BF16).astype(F32)
    rest = depth - 3 * x.shape[0]
    parts = [x, low, x]
    if rest:
        parts.append(jnp.zeros((rest, x.shape[1]), F32))
    return jnp.concatenate(parts, axis=0).astype(BF16)


def twice(x):
    return jnp.concatenate([x, x], axis=0)


def grow(x, rows):
    if rows == x.shape[0]:
        return x
    return jnp.concatenate([x, jnp.zeros((rows - x.shape[0], x.shape[1]), F32)], axis=0)


def row_of(ref, *lead_and_row):
    lead, row = lead_and_row[:-1], lead_and_row[-1]
    return ref[(*lead, pl.ds(row, 1), slice(None))]


def at_columns(rows, columns, test):
    row = lax.broadcasted_iota(jnp.int32, (rows, columns), 0)
    column = lax.broadcasted_iota(jnp.int32, (rows, columns), 1)
    return jnp.where(test(row, column), 1.0, 0.0).astype(BF16)


def shifted(rows, columns, shift):
    return at_columns(rows, columns, lambda row, column: column == row + shift)


def columns3(w, depth):
    hi, lo = split(w)
    inner = w.shape[1]
    first = at_columns(inner, depth, lambda r, c: (c == r) | (c == r + inner))
    return (dot(hi, first) + dot(lo, shifted(inner, depth, 2 * inner))).astype(BF16)


def kernel(
    sizes,
    state_hbm,
    star_hbm,
    flux_hbm,
    stiff_hbm,
    vol_hbm,
    proj_hbm,
    lift_hbm,
    maps_hbm,
    near_idx_ref,
    orient_ref,
    slots_ref,
    count_ref,
    out_ref,
    star_ref,
    flux_ref,
    stiff_ref,
    vol_ref,
    proj_ref,
    lift_ref,
    maps_ref,
    load_sem,
    star_pair,
    y_even,
    y_odd,
    pair_even,
    pair_odd,
    part,
    part_pair,
    taylor,
    slow,
    part_rows,
    trace,
    table,
    near,
    remote,
    pred_w,
    vol_w,
    proj_w,
    own_w,
    near_w,
    hot_local,
    hot_remote,
    hot_send,
    mask,
    send,
    recv,
    send_sem,
    recv_sem,
    forward_sem,
):
    n_dom, n_sub, modes, fields, face_pad, slots = sizes
    faces = 4
    face_modes = maps_ref.shape[1]
    half = LANES // 2
    pairs = (fields + 1) // 2
    depth = pred_w.shape[1]
    mode_pad = up(modes, 16)
    fold = LANES // slots
    table_rows = table.shape[0]
    fold_rows = table_rows // fold
    group = n_sub * slots
    face_rows = faces * face_pad
    own_count = faces * LANES
    loads = [
        pltpu.make_async_copy(source, target, load_sem.at[i])
        for i, (source, target) in enumerate(
            [
                (stiff_hbm, stiff_ref),
                (state_hbm, out_ref),
                (star_hbm, star_ref),
                (proj_hbm, proj_ref),
                (vol_hbm, vol_ref),
                (lift_hbm, lift_ref),
                (maps_hbm, maps_ref),
                (flux_hbm, flux_ref),
            ]
        )
    ]
    for load in loads:
        load.start()
    dom, sub = lax.axis_index("dom"), lax.axis_index("sub")
    has_low, has_high = dom > 0, dom < n_dom - 1

    barrier = pltpu.get_barrier_semaphore()

    def greet(d, s):
        pl.semaphore_signal(
            barrier, inc=1, device_id={"dom": d, "sub": s}, device_id_type=pl.DeviceIdType.MESH
        )

    chips = n_sub // 2
    chip, core = sub // 2, lax.rem(sub, 2)
    sibling = 2 * chip + 1 - core

    greet(dom, sibling)
    for k in range(1, chips):
        greet(dom, 2 * lax.rem(chip + k, chips) + core)

    @pl.when(has_low)
    def _():
        for c in range(chips):
            greet(dom - 1, 2 * c + core)

    @pl.when(has_high)
    def _():
        for c in range(chips):
            greet(dom + 1, 2 * c + core)

    @pl.when(jnp.logical_not(has_low))
    def _():
        recv[:, 1] = jnp.zeros((2, *recv.shape[2:]), F32)

    @pl.when(jnp.logical_not(has_high))
    def _():
        recv[:, 2] = jnp.zeros((2, *recv.shape[2:]), F32)

    def one_hot(row, rows):
        at = lax.broadcasted_iota(jnp.int32, (rows, LANES), 0)
        return jnp.where(at == row, 1.0, 0.0).astype(BF16)

    tiled = dot(
        stacked(grow(slots_ref[...].astype(F32), 8)),
        at_columns(slots, LANES, lambda row, column: column % slots == row),
    )
    tiled = (tiled[:8] + tiled[8:]).astype(jnp.int32)
    for i in range(2):
        hot_send[:, i * LANES : (i + 1) * LANES] = one_hot(tiled[i : i + 1, :], own_count)

    def by_direction(ref):
        rows = jnp.concatenate([ref[d] for d in range(3)], axis=0)
        return grow(rows, pred_w.shape[0])

    def by_face(ref):
        return jnp.concatenate([grow(ref[:, j, :], face_pad) for j in range(faces)], axis=0)

    loads[0].wait()
    pred_w[...] = columns3(-by_direction(stiff_ref), depth)

    chunks = [tuple(range(f, min(f + 2, fields))) for f in range(0, fields, 2)]
    pair_chunks = [tuple(range(i, min(i + 2, pairs))) for i in range(0, pairs, 2)]

    def cols(chunk):
        return slice(chunk[0] * LANES, (chunk[-1] + 1) * LANES)

    def lane(i):
        return slice(i * LANES, (i + 1) * LANES)

    def side_by_side(values):
        return values[0] if len(values) == 1 else jnp.concatenate(values, axis=1)

    def stiff_rows(value):
        return dot(pred_w[...], rows3(value, depth))[: 3 * modes]

    blocks = [(start, min(16, modes - start)) for start in range(0, modes, 16)]

    def contract(source, terms, rows, targets):
        values = [[] for _ in targets]
        for start, count in blocks:
            totals = [[None] * 3 for _ in targets]
            for g in range(terms):
                for d in range(3):
                    first = d * modes + start
                    item = source[first : first + count, lane(g)]
                    for i, f in enumerate(targets):
                        term = row_of(rows, f, g, d) * item
                        total = totals[i][d]
                        totals[i][d] = term if total is None else total + term
            for i, total in enumerate(totals):
                values[i].append(total[0] + total[1] + total[2])
        return [jnp.concatenate(value, axis=0) for value in values]

    low_half = lax.broadcasted_iota(jnp.int32, (modes, LANES), 1) < half

    def pair_up(first, second):
        return jnp.where(low_half, first, pltpu.roll(second, half, 1))

    def contract_pairs(source, chunk):
        targets = [f for i in chunk for f in (2 * i, 2 * i + 1) if f < fields]
        values = contract(source, pairs, star_pair, targets)
        if len(targets) < 2 * len(chunk):
            values.append(jnp.zeros((modes, LANES), F32))
        result = []
        for i in range(len(chunk)):
            even, odd = values[2 * i], values[2 * i + 1]
            result.append(
                jnp.where(low_half, even, odd)
                + pltpu.roll(jnp.where(low_half, odd, even), half, 1)
            )
        return side_by_side(result)

    def project(chunk, value):
        rows = rows3(value, depth)
        part_rows[:, cols(chunk)] = rows
        value = dot(proj_w[...], rows)
        for i, g in enumerate(chunk):
            for j in range(faces):
                trace[j, g * face_modes : g * face_modes + face_pad, :] = value[
                    j * face_pad : (j + 1) * face_pad, lane(i)
                ]

    def flux_rows(side, src, chunk):
        found = [[] for _ in chunk]
        for j in range(faces):
            totals = [None] * len(chunk)
            for g in range(fields):
                item = src[j, g * face_modes : g * face_modes + face_pad, :]
                for i, f in enumerate(chunk):
                    term = row_of(flux_ref, side, f, g, j) * item
                    totals[i] = term if totals[i] is None else totals[i] + term
            for i, total in enumerate(totals):
                found[i].append(total)
        return [jnp.concatenate(value, axis=0) for value in found]

    def add_out(chunk, value):
        for i, f in enumerate(chunk):
            out_ref[f] = out_ref[f] + value[:modes, lane(i)]

    def out_copy(ex, which, target, region, at):
        return pltpu.make_async_remote_copy(
            src_ref=send.at[ex, which],
            dst_ref=recv.at[ex, region, sub],
            send_sem=send_sem.at[ex, region, at],
            recv_sem=recv_sem.at[ex, region, sub],
            device_id=target,
            device_id_type=pl.DeviceIdType.MESH,
        )

    def exchange_copies(ex):
        inner = [out_copy(ex, 0, {"dom": dom, "sub": sibling}, 0, 0)]
        for k in range(1, chips):
            target = {"dom": dom, "sub": 2 * lax.rem(chip + k, chips) + core}
            inner.append(out_copy(ex, 0, target, 0, k))
        lower = [
            out_copy(ex, 1, {"dom": dom - 1, "sub": 2 * c + core}, 2, c) for c in range(chips)
        ]
        upper = [
            out_copy(ex, 1, {"dom": dom + 1, "sub": 2 * c + core}, 1, c) for c in range(chips)
        ]
        return inner, lower, upper

    def arrival(ex, region, s):
        return pltpu.make_async_remote_copy(
            src_ref=send.at[ex, 0],
            dst_ref=recv.at[ex, region, s],
            send_sem=send_sem.at[ex, region, 0],
            recv_sem=recv_sem.at[ex, region, s],
            device_id={"dom": dom, "sub": sub},
            device_id_type=pl.DeviceIdType.MESH,
        )

    def forward(ex, region, s):
        return pltpu.make_async_remote_copy(
            src_ref=recv.at[ex, region, s],
            dst_ref=recv.at[ex, region, s],
            send_sem=forward_sem.at[ex, region, s],
            recv_sem=recv_sem.at[ex, region, s],
            device_id={"dom": dom, "sub": sibling},
            device_id_type=pl.DeviceIdType.MESH,
        )

    def each_region(do, side):
        @pl.when(has_low)
        def _():
            for c in range(chips):
                do(1, 2 * c + side)

        @pl.when(has_high)
        def _():
            for c in range(chips):
                do(2, 2 * c + side)

        for k in range(1, chips):
            do(0, 2 * lax.rem(chip + k, chips) + side)

    section = lax.broadcasted_iota(jnp.int32, (fold_rows, LANES), 1) // slots

    def send_traces(ex):
        for j in range(faces):
            hi, lo = split(trace[j])
            table[:, lane(j)] = hi
            table[:, lane(faces + j)] = lo
        picked = dot(table[...], twice(hot_send[...]))
        for i in range(2):
            packed = picked[:fold_rows, lane(i)]
            for a in range(1, fold):
                packed = jnp.where(
                    section == a, picked[a * fold_rows : (a + 1) * fold_rows, lane(i)], packed
                )
            send[ex, i] = packed
            if i == 0:
                recv[ex, 0, sub] = packed
        if ex == 0:
            pl.semaphore_wait(
                barrier, chips * (1 + has_low.astype(jnp.int32) + has_high.astype(jnp.int32))
            )
        inner, lower, upper = exchange_copies(ex)

        @pl.when(has_low)
        def _():
            for copy in lower:
                copy.start()

        @pl.when(has_high)
        def _():
            for copy in upper:
                copy.start()

        for copy in inner:
            copy.start()

    def own_update():
        for jj in range(0, faces, 2):
            at = slice(jj * LANES, (jj + 2) * LANES)
            found = dot(table[...], twice(hot_local[:, at]))
            near[jj] = found[:, :LANES]
            near[jj + 1] = found[:, LANES:]
        for chunk in chunks:
            y_even[:, cols(chunk)] = dot(vol_w[...], part_rows[:, cols(chunk)])[: 3 * modes]
        for chunk in chunks:
            volume = side_by_side(contract(y_even, fields, star_ref, chunk))
            own = side_by_side(flux_rows(0, trace, chunk))
            add_out(chunk, volume + dot(own_w[...], rows3(own, 3 * face_rows))[:modes])

    def take_arrivals(ex):
        def pass_on(region, s):
            arrival(ex, region, s).wait_recv()
            forward(ex, region, s).start()

        each_region(pass_on, core)
        arrival(ex, 0, sibling).wait_recv()
        each_region(lambda region, s: arrival(ex, region, s).wait_recv(), 1 - core)

        for region in range(3):
            for b in range(n_sub // fold):
                parts = [recv[ex, region, b * fold + i] for i in range(fold)]
                for a in range(fold):
                    value = None
                    for i in range(fold):
                        moved = parts[i]
                        if i != a:
                            moved = pltpu.roll(moved, ((i - a) * slots) % LANES, 1)
                        value = moved if value is None else jnp.where(section == i, moved, value)
                    first = region * group + b * LANES
                    rows = slice(a * fold_rows, (a + 1) * fold_rows)
                    hi, lo = split(value)
                    remote[rows, first : first + LANES] = hi
                    first = first + 3 * group
                    remote[rows, first : first + LANES] = lo

    def near_update():
        for jj in range(0, faces, 2):
            at = slice(jj * LANES, (jj + 2) * LANES)
            found = dot(remote[...], twice(hot_remote[:, at]))
            near[jj] = near[jj] + found[:, :LANES]
            near[jj + 1] = near[jj + 1] + found[:, LANES:]
        masks = [mask[o].astype(BF16) for o in range(3)]
        for chunk in chunks:
            pieces = []
            for value in flux_rows(1, near, chunk):
                hi, lo = split(value)
                hi = [hi * masks[o] for o in range(3)]
                lo = [lo * masks[o] for o in range(3)]
                pieces.append(jnp.concatenate(hi + lo + hi, axis=0))
            add_out(chunk, dot(near_w[...], side_by_side(pieces)))

    def finish_sends(ex):
        inner, lower, upper = exchange_copies(ex)
        for copy in inner:
            copy.wait_send()

        @pl.when(has_low)
        def _():
            for copy in lower:
                copy.wait_send()

        @pl.when(has_high)
        def _():
            for copy in upper:
                copy.wait_send()

        each_region(lambda region, s: forward(ex, region, s).wait_send(), core)

    def prepare_update():
        for j in range(faces):
            row = near_idx_ref[j : j + 1, :]
            hot_local[:, lane(j)] = one_hot(row, own_count)
            hot_remote[:, lane(j)] = one_hot(row - own_count, 3 * group)
            turn = orient_ref[j : j + 1, :]
            for o in range(3):
                mask[o, j * face_pad : (j + 1) * face_pad, :] = jnp.broadcast_to(
                    jnp.where(turn == o, 1.0, 0.0), (face_pad, LANES)
                )
        vol_w[...] = columns3(by_direction(vol_ref), depth)
        same = shifted(mode_pad, modes, 0)
        lift = []
        for value in split(-by_face(lift_ref)):
            lift.append(
                lax.dot_general(same, value, (((1,), (1,)), ((), ())), preferred_element_type=F32)
            )
        hi, lo = lift[0].astype(BF16), lift[1].astype(BF16)
        own_w[:, :face_rows] = hi
        own_w[:, face_rows : 2 * face_rows] = hi
        own_w[:, 2 * face_rows :] = lo
        turned = None
        map_pad = up(face_pad, 16)
        for o in range(3):
            place = at_columns(
                face_modes,
                3 * face_rows,
                lambda row, column: (column // face_rows == o) & (column % face_pad == row),
            )
            both = dot(stacked(grow(maps_ref[o], map_pad)), place)
            term = both[:face_pad] + both[map_pad : map_pad + face_pad]
            turned = term if turned is None else turned + term
        turned = jnp.concatenate([turned] * faces, axis=0)
        row = lax.broadcasted_iota(jnp.int32, turned.shape, 0)
        column = lax.broadcasted_iota(jnp.int32, turned.shape, 1)
        turned = jnp.where(column % face_rows // face_pad == row // face_pad, turned, 0.0)
        turned_hi, turned_lo = split(turned)
        value = dot(hi, turned_hi) + dot(lo, turned_hi) + dot(hi, turned_lo)
        hi, lo = split(value)
        near_w[:, : 3 * face_rows] = hi
        near_w[:, 3 * face_rows : 6 * face_rows] = hi
        near_w[:, 6 * face_rows :] = lo

    def prepare_pairs():
        low = lax.broadcasted_iota(jnp.int32, (8, LANES), 1) < half
        for f in range(fields):
            for i in range(pairs):
                first = grow(star_ref[f, 2 * i], 8)
                if 2 * i + 1 < fields:
                    second = pltpu.roll(grow(star_ref[f, 2 * i + 1], 8), half, 1)
                else:
                    second = jnp.zeros((8, LANES), F32)
                star_pair[f, i] = jnp.where(low, first, second)[:3]

    def sum_slow():
        for f in range(fields):
            total = part[:, lane(f)]
            weight = 1.0
            for k in range(DEGREE):
                weight = weight / (k + 2)
                total = total + ((2.0 ** (k + 2) - 2.0) * weight) * taylor[k, :, lane(f)]
            slow[:, lane(f)] = total

    loads[1].wait()
    for chunk in chunks:
        value = side_by_side([out_ref[f] for f in chunk])
        part[:, cols(chunk)] = value
        y_even[:, cols(chunk)] = stiff_rows(value)
    loads[2].wait()

    def order(k, weight, source, target):
        weight = weight / (k.astype(F32) + 2.0)
        for chunk in chunks:
            value = side_by_side(contract(source, fields, star_ref, chunk))
            taylor[k, :, cols(chunk)] = value
            part[:, cols(chunk)] = part[:, cols(chunk)] + weight * value
            target[:, cols(chunk)] = stiff_rows(value)
        return weight

    def two_orders(k, weight):
        weight = order(2 * k, weight, y_even, y_odd)
        return order(2 * k + 1, weight, y_odd, y_even)

    weight = lax.fori_loop(0, DEGREE // 2, two_orders, jnp.float32(1.0)) / (DEGREE + 1.0)
    loads[3].wait()
    proj_w[...] = columns3(by_face(proj_ref), depth)
    for chunk in chunks:
        value = side_by_side(contract(y_even, fields, star_ref, chunk))
        taylor[DEGREE - 1, :, cols(chunk)] = value
        value = part[:, cols(chunk)] + weight * value
        part[:, cols(chunk)] = value
        project(chunk, value)
    send_traces(0)

    for load in loads[4:]:
        load.wait()
    prepare_update()
    own_update()
    prepare_pairs()
    sum_slow()
    take_arrivals(0)
    near_update()
    finish_sends(0)

    for chunk in pair_chunks:
        value = []
        for i in chunk:
            first = out_ref[2 * i]
            second = out_ref[min(2 * i + 1, fields - 1)]
            value.append(pair_up(first, second))
        value = side_by_side(value)
        part_pair[:, cols(chunk)] = value
        pair_even[:, cols(chunk)] = stiff_rows(value)

    def pair_order(k, weight, source, target):
        weight = weight / (k.astype(F32) + 2.0)
        for chunk in pair_chunks:
            value = contract_pairs(source, chunk)
            part_pair[:, cols(chunk)] = part_pair[:, cols(chunk)] + weight * value
            target[:, cols(chunk)] = stiff_rows(value)
        return weight

    def two_pair_orders(k, weight):
        weight = pair_order(2 * k, weight, pair_even, pair_odd)
        return pair_order(2 * k + 1, weight, pair_odd, pair_even)

    weight = lax.fori_loop(0, DEGREE // 2, two_pair_orders, jnp.float32(1.0)) / (DEGREE + 1.0)
    is_fast = lax.broadcasted_iota(jnp.int32, (modes, LANES), 1) < count_ref[0]
    for chunk in pair_chunks:
        value = part_pair[:, cols(chunk)] + weight * contract_pairs(pair_even, chunk)
        for n, i in enumerate(chunk):
            item = value[:, lane(n)]
            both = [item, pltpu.roll(item, half, 1)]
            mine = tuple(f for f in (2 * i, 2 * i + 1) if f < fields)
            mixed = [
                jnp.where(is_fast, both[q], slow[:, lane(f)]) for q, f in enumerate(mine)
            ]
            project(mine, side_by_side(mixed))
    send_traces(1)
    own_update()
    take_arrivals(1)
    near_update()
    finish_sends(1)


def local(
    n_dom,
    n_sub,
    modal_state,
    star_mats,
    face_flux,
    stiffness,
    stiff_vol,
    face_proj,
    face_lifting_matrix,
    orient_maps,
    neighbours,
    face_orient,
    send_slots,
    fast_count,
):
    modes, fields, elems = modal_state.shape
    face_modes = orient_maps.shape[1]
    slots = send_slots.shape[1]
    fold = LANES // slots
    face_pad, mode_pad = up(face_modes, 8), up(modes, 16)
    table_rows = up((fields - 1) * face_modes + face_pad, 8 * fold)
    group = n_sub * slots
    width = fields * elems
    pairs = (fields + 1) // 2
    depth, rows3 = up(3 * modes, 16), up(3 * modes, 16)
    face_rows = 4 * face_pad
    any_space = pl.BlockSpec(memory_space=pl.ANY)
    vmem = pl.BlockSpec(memory_space=pltpu.VMEM)
    out = pl.pallas_call(
        functools.partial(kernel, (n_dom, n_sub, modes, fields, face_pad, slots)),
        out_shape=jax.ShapeDtypeStruct((fields, modes, elems), F32),
        in_specs=[any_space] * 8 + [vmem] * 3 + [pl.BlockSpec(memory_space=pltpu.SMEM)],
        out_specs=vmem,
        scratch_shapes=[
            pltpu.VMEM((fields, fields, 3, elems), F32),
            pltpu.VMEM((2, fields, fields, 4, elems), F32),
            pltpu.VMEM((3, modes, modes), F32),
            pltpu.VMEM((3, modes, modes), F32),
            pltpu.VMEM((face_modes, 4, modes), F32),
            pltpu.VMEM((face_modes, 4, modes), F32),
            pltpu.VMEM((3, face_modes, face_modes), F32),
            pltpu.SemaphoreType.DMA((8,)),
            pltpu.VMEM((fields, pairs, 3, elems), F32),
            pltpu.VMEM((3 * modes, width), F32),
            pltpu.VMEM((3 * modes, width), F32),
            pltpu.VMEM((3 * modes, pairs * elems), F32),
            pltpu.VMEM((3 * modes, pairs * elems), F32),
            pltpu.VMEM((modes, width), F32),
            pltpu.VMEM((modes, pairs * elems), F32),
            pltpu.VMEM((DEGREE, modes, width), F32),
            pltpu.VMEM((modes, width), F32),
            pltpu.VMEM((depth, width), BF16),
            pltpu.VMEM((4, table_rows, elems), F32),
            pltpu.VMEM((table_rows, 8 * elems), BF16),
            pltpu.VMEM((4, table_rows, elems), F32),
            pltpu.VMEM((table_rows, 6 * group), BF16),
            pltpu.VMEM((rows3, depth), BF16),
            pltpu.VMEM((rows3, depth), BF16),
            pltpu.VMEM((face_rows, depth), BF16),
            pltpu.VMEM((mode_pad, 3 * face_rows), BF16),
            pltpu.VMEM((mode_pad, 9 * face_rows), BF16),
            pltpu.VMEM((4 * elems, 4 * elems), BF16),
            pltpu.VMEM((3 * group, 4 * elems), BF16),
            pltpu.VMEM((4 * elems, 2 * LANES), BF16),
            pltpu.VMEM((3, face_rows, LANES), F32),
            pltpu.VMEM((2, 2, table_rows // fold, LANES), F32),
            pltpu.VMEM((2, 3, n_sub, table_rows // fold, LANES), F32),
            pltpu.SemaphoreType.DMA((2, 3, n_sub)),
            pltpu.SemaphoreType.DMA((2, 3, n_sub)),
            pltpu.SemaphoreType.DMA((2, 3, n_sub)),
        ],
        compiler_params=pltpu.CompilerParams(collective_id=0, has_side_effects=True),
    )(
        modal_state.transpose(1, 0, 2),
        star_mats.transpose(1, 2, 0, 3),
        face_flux.transpose(0, 2, 3, 1, 4),
        stiffness,
        stiff_vol,
        face_proj.transpose(2, 0, 1),
        face_lifting_matrix.transpose(1, 0, 2),
        orient_maps,
        neighbours,
        face_orient,
        send_slots,
        fast_count,
    )
    return out.transpose(1, 0, 2)


def solution(mesh):
    split_last = ("dom", "sub")
    placed = (
        P(None, None, split_last),
        P(None, None, None, split_last),
        P(None, None, None, None, split_last),
        P(),
        P(),
        P(),
        P(),
        P(),
        P(None, split_last),
        P(None, split_last),
        P(None, split_last),
        P(split_last),
    )
    return jax.shard_map(
        functools.partial(local, mesh.shape["dom"], mesh.shape["sub"]),
        mesh=mesh,
        in_specs=placed,
        out_specs=P(None, None, split_last),
        check_vma=False,
    )
```

time: 28.7 us -> 26.2 us (0.913)
  Pallas kernels: 26.2 us -> 23.7 us
    pallas_call x1, Pallas kernels: 26.2 us -> 23.7 us  [local(): pl.pallas_call(functools.partial(kernel, (n_dom, n_sub, modes, fields, fa...]
where the time goes in v1:
time: 26.2 us; the launch traced here: 26 us
  Pallas kernels  23.7 us (90%)
  local copies, waits for them, and re-layouts  1.66 us (6%)
  between operations  0.66 us (3%)
    pallas_call x1, Pallas kernels, local(): pl.pallas_call(functools.partial(kernel, (n_dom, n_sub, modes, fields, fa...  23.7 us
    unnamed x1, local copies, waits for them, and re-layouts  1.66 us

profile of v1, /device:TPU:21, one launch (start us, length us, event | category | flops | bytes accessed | tf_op | source)
XLA Modules:
  0.0 26.0 jit_solution(13309607175225697797)
XLA Ops:
  0.7 23.7 %shard_map.118 = f32[9,56,128]{2,1,0:T(8,128)} custom-call(f32[9,56,128]{2,1,0:T(8,128)} %bitcast.8, f32[9,9,3,128]{3,2,1,0:T(4,128)} %bitcast.9, f32[2,9,9,4,128]{4,3,2,1,0:T(4,128)} %bitcast.7, f32[3,56,56]{2,1,0:T(8,128)} %stiff_hbm.1, f32[3,56,56]{2,1,0:T(8,128)} %vol_hbm.1, f32[21,4,56]{2,1,0:T(4,128)} %bitcast.10, f32[21,4,56]{2,1,0:T(4,128)} %bitcast.11, ...), custom_call_target="tpu_custom_call" | custom-call | tf_op jit(solution)/shard_map/pallas_call | solution.py:633
  24.3 1.7 %copy.15 = f32[56,9,128]{2,0,1:T(8,128)} copy(f32[56,9,128]{2,0,1:T(8,128)} %bitcast.6) | data formatting | bytes 516096

commit v2 on v1

--- a/solution.py
+++ b/solution.py
@@ -108,6 +108,7 @@
     trace,
     table,
     near,
+    near_flux,
     remote,
     pred_w,
     vol_w,
@@ -118,11 +119,10 @@
     hot_remote,
     hot_send,
     mask,
-    send,
-    recv,
     send_sem,
     recv_sem,
     forward_sem,
+    *buffers,
 ):
     n_dom, n_sub, modes, fields, face_pad, slots = sizes
     faces = 4
@@ -132,8 +132,16 @@
     depth = pred_w.shape[1]
     mode_pad = up(modes, 16)
     fold = LANES // slots
-    table_rows = table.shape[0]
-    fold_rows = table_rows // fold
+    pair_chunks = [tuple(range(i, min(i + 2, pairs))) for i in range(0, pairs, 2)]
+    parcels = [tuple(f for i in c for f in (2 * i, 2 * i + 1) if f < fields) for c in pair_chunks]
+    count = len(parcels)
+    sends, recvs = buffers[:count], buffers[count:]
+    sizes = [fold * ref.shape[-2] for ref in sends]
+    firsts = [sum(sizes[:q]) for q in range(count)]
+    field_row = {
+        f: firsts[q] + i * face_modes for q, p in enumerate(parcels) for i, f in enumerate(p)
+    }
+    straight = count - 1
     group = n_sub * slots
     face_rows = faces * face_pad
     own_count = faces * LANES
@@ -168,27 +176,33 @@
     chip, core = sub // 2, lax.rem(sub, 2)
     sibling = 2 * chip + 1 - core
 
-    greet(dom, sibling)
-    for k in range(1, chips):
-        greet(dom, 2 * lax.rem(chip + k, chips) + core)
+    for k in range(1, n_sub):
+        greet(dom, lax.rem(sub + k, n_sub))
 
     @pl.when(has_low)
     def _():
-        for c in range(chips):
-            greet(dom - 1, 2 * c + core)
+        for c in range(n_sub):
+            greet(dom - 1, c)
 
     @pl.when(has_high)
     def _():
-        for c in range(chips):
-            greet(dom + 1, 2 * c + core)
+        for c in range(n_sub):
+            greet(dom + 1, c)
 
     @pl.when(jnp.logical_not(has_low))
     def _():
-        recv[:, 1] = jnp.zeros((2, *recv.shape[2:]), F32)
+        for recv in recvs:
+            recv[:, 1] = jnp.zeros((2, *recv.shape[2:]), F32)
 
     @pl.when(jnp.logical_not(has_high))
     def _():
-        recv[:, 2] = jnp.zeros((2, *recv.shape[2:]), F32)
+        for recv in recvs:
+            recv[:, 2] = jnp.zeros((2, *recv.shape[2:]), F32)
+
+    for q, fields_of in enumerate(parcels):
+        used = firsts[q] + len(fields_of) * face_modes
+        end = firsts[q] + sizes[q]
+        trace[:, used:end, :] = jnp.zeros((faces, end - used, LANES), F32)
 
     def one_hot(row, rows):
         at = lax.broadcasted_iota(jnp.int32, (rows, LANES), 0)
@@ -213,7 +227,6 @@
     pred_w[...] = columns3(-by_direction(stiff_ref), depth)
 
     chunks = [tuple(range(f, min(f + 2, fields))) for f in range(0, fields, 2)]
-    pair_chunks = [tuple(range(i, min(i + 2, pairs))) for i in range(0, pairs, 2)]
 
     def cols(chunk):
         return slice(chunk[0] * LANES, (chunk[-1] + 1) * LANES)
@@ -270,16 +283,17 @@
         value = dot(proj_w[...], rows)
         for i, g in enumerate(chunk):
             for j in range(faces):
-                trace[j, g * face_modes : g * face_modes + face_pad, :] = value[
+                trace[j, field_row[g] : field_row[g] + face_pad, :] = value[
                     j * face_pad : (j + 1) * face_pad, lane(i)
                 ]
 
-    def flux_rows(side, src, chunk):
+    def flux_rows(side, src, chunk, given, starts=None):
         found = [[] for _ in chunk]
         for j in range(faces):
-            totals = [None] * len(chunk)
-            for g in range(fields):
-                item = src[j, g * face_modes : g * face_modes + face_pad, :]
+            block = slice(j * face_pad, (j + 1) * face_pad)
+            totals = [None if starts is None else starts[f, block, :] for f in chunk]
+            for g in given:
+                item = src[j, field_row[g] : field_row[g] + face_pad, :]
                 for i, f in enumerate(chunk):
                     term = row_of(flux_ref, side, f, g, j) * item
                     totals[i] = term if totals[i] is None else totals[i] + term
@@ -291,50 +305,57 @@
         for i, f in enumerate(chunk):
             out_ref[f] = out_ref[f] + value[:modes, lane(i)]
 
-    def out_copy(ex, which, target, region, at):
+    def out_copy(ex, q, which, target, region, at):
         return pltpu.make_async_remote_copy(
-            src_ref=send.at[ex, which],
-            dst_ref=recv.at[ex, region, sub],
-            send_sem=send_sem.at[ex, region, at],
-            recv_sem=recv_sem.at[ex, region, sub],
+            src_ref=sends[q].at[ex, which],
+            dst_ref=recvs[q].at[ex, region, sub],
+            send_sem=send_sem.at[ex, q, region, at],
+            recv_sem=recv_sem.at[ex, q, region, sub],
             device_id=target,
             device_id_type=pl.DeviceIdType.MESH,
         )
 
-    def exchange_copies(ex):
-        inner = [out_copy(ex, 0, {"dom": dom, "sub": sibling}, 0, 0)]
-        for k in range(1, chips):
-            target = {"dom": dom, "sub": 2 * lax.rem(chip + k, chips) + core}
-            inner.append(out_copy(ex, 0, target, 0, k))
-        lower = [
-            out_copy(ex, 1, {"dom": dom - 1, "sub": 2 * c + core}, 2, c) for c in range(chips)
-        ]
-        upper = [
-            out_copy(ex, 1, {"dom": dom + 1, "sub": 2 * c + core}, 1, c) for c in range(chips)
-        ]
+    def exchange_copies(ex, q):
+        if q == straight:
+            inner = [
+                out_copy(ex, q, 0, {"dom": dom, "sub": lax.rem(sub + k, n_sub)}, 0, k)
+                for k in range(1, n_sub)
+            ]
+            beside = [(c, c) for c in range(n_sub)]
+        else:
+            inner = [out_copy(ex, q, 0, {"dom": dom, "sub": sibling}, 0, 0)]
+            for k in range(1, chips):
+                target = {"dom": dom, "sub": 2 * lax.rem(chip + k, chips) + core}
+                inner.append(out_copy(ex, q, 0, target, 0, k))
+            beside = [(2 * c + core, c) for c in range(chips)]
+        lower = [out_copy(ex, q, 1, {"dom": dom - 1, "sub": s}, 2, at) for s, at in beside]
+        upper = [out_copy(ex, q, 1, {"dom": dom + 1, "sub": s}, 1, at) for s, at in beside]
         return inner, lower, upper
 
-    def arrival(ex, region, s):
+    def arrival(ex, q, region, s):
         return pltpu.make_async_remote_copy(
-            src_ref=send.at[ex, 0],
-            dst_ref=recv.at[ex, region, s],
-            send_sem=send_sem.at[ex, region, 0],
-            recv_sem=recv_sem.at[ex, region, s],
+            src_ref=sends[q].at[ex, 0],
+            dst_ref=recvs[q].at[ex, region, s],
+            send_sem=send_sem.at[ex, q, region, 0],
+            recv_sem=recv_sem.at[ex, q, region, s],
             device_id={"dom": dom, "sub": sub},
             device_id_type=pl.DeviceIdType.MESH,
         )
 
-    def forward(ex, region, s):
+    def forward(ex, q, region, s):
         return pltpu.make_async_remote_copy(
-            src_ref=recv.at[ex, region, s],
-            dst_ref=recv.at[ex, region, s],
-            send_sem=forward_sem.at[ex, region, s],
-            recv_sem=recv_sem.at[ex, region, s],
+            src_ref=recvs[q].at[ex, region, s],
+            dst_ref=recvs[q].at[ex, region, s],
+            send_sem=forward_sem.at[ex, q, region, s],
+            recv_sem=recv_sem.at[ex, q, region, s],
             device_id={"dom": dom, "sub": sibling},
             device_id_type=pl.DeviceIdType.MESH,
         )
 
     def each_region(do, side):
+        for k in range(1, chips):
+            do(0, 2 * lax.rem(chip + k, chips) + side)
+
         @pl.when(has_low)
         def _():
             for c in range(chips):
@@ -345,31 +366,30 @@
             for c in range(chips):
                 do(2, 2 * c + side)
 
-        for k in range(1, chips):
-            do(0, 2 * lax.rem(chip + k, chips) + side)
-
-    section = lax.broadcasted_iota(jnp.int32, (fold_rows, LANES), 1) // slots
-
-    def send_traces(ex):
+    def gather(ex, q):
+        rows = slice(firsts[q], firsts[q] + sizes[q])
         for j in range(faces):
-            hi, lo = split(trace[j])
-            table[:, lane(j)] = hi
-            table[:, lane(faces + j)] = lo
-        picked = dot(table[...], twice(hot_send[...]))
+            hi, lo = split(trace[j, rows, :])
+            table[rows, lane(j)] = hi
+            table[rows, lane(faces + j)] = lo
+        picked = dot(table[rows, :], twice(hot_send[...]))
+        fold_rows = sizes[q] // fold
+        section = lax.broadcasted_iota(jnp.int32, (fold_rows, LANES), 1) // slots
         for i in range(2):
             packed = picked[:fold_rows, lane(i)]
             for a in range(1, fold):
                 packed = jnp.where(
                     section == a, picked[a * fold_rows : (a + 1) * fold_rows, lane(i)], packed
                 )
-            send[ex, i] = packed
+            sends[q][ex, i] = packed
             if i == 0:
-                recv[ex, 0, sub] = packed
-        if ex == 0:
-            pl.semaphore_wait(
-                barrier, chips * (1 + has_low.astype(jnp.int32) + has_high.astype(jnp.int32))
-            )
-        inner, lower, upper = exchange_copies(ex)
+                recvs[q][ex, 0, sub] = packed
+
+    def start(ex, q):
+        if ex == 0 and q == 0:
+            sides = has_low.astype(jnp.int32) + has_high.astype(jnp.int32)
+            pl.semaphore_wait(barrier, n_sub - 1 + n_sub * sides)
+        inner, lower, upper = exchange_copies(ex, q)
 
         @pl.when(has_low)
         def _():
@@ -394,21 +414,15 @@
             y_even[:, cols(chunk)] = dot(vol_w[...], part_rows[:, cols(chunk)])[: 3 * modes]
         for chunk in chunks:
             volume = side_by_side(contract(y_even, fields, star_ref, chunk))
-            own = side_by_side(flux_rows(0, trace, chunk))
+            own = side_by_side(flux_rows(0, trace, chunk, range(fields)))
             add_out(chunk, volume + dot(own_w[...], rows3(own, 3 * face_rows))[:modes])
 
-    def take_arrivals(ex):
-        def pass_on(region, s):
-            arrival(ex, region, s).wait_recv()
-            forward(ex, region, s).start()
-
-        each_region(pass_on, core)
-        arrival(ex, 0, sibling).wait_recv()
-        each_region(lambda region, s: arrival(ex, region, s).wait_recv(), 1 - core)
-
+    def unpack(ex, q):
+        fold_rows = sizes[q] // fold
+        section = lax.broadcasted_iota(jnp.int32, (fold_rows, LANES), 1) // slots
         for region in range(3):
             for b in range(n_sub // fold):
-                parts = [recv[ex, region, b * fold + i] for i in range(fold)]
+                parts = [recvs[q][ex, region, b * fold + i] for i in range(fold)]
                 for a in range(fold):
                     value = None
                     for i in range(fold):
@@ -417,22 +431,42 @@
                             moved = pltpu.roll(moved, ((i - a) * slots) % LANES, 1)
                         value = moved if value is None else jnp.where(section == i, moved, value)
                     first = region * group + b * LANES
-                    rows = slice(a * fold_rows, (a + 1) * fold_rows)
-                    hi, lo = split(value)
-                    remote[rows, first : first + LANES] = hi
-                    first = first + 3 * group
-                    remote[rows, first : first + LANES] = lo
-
-    def near_update():
+                    rows = slice(firsts[q] + a * fold_rows, firsts[q] + (a + 1) * fold_rows)
+                    remote[rows, first : first + LANES] = value
+
+    def add_near(q):
+        rows = slice(firsts[q], firsts[q] + sizes[q])
+        hi, lo = split(remote[rows, :])
+        both = jnp.concatenate([hi, lo], axis=1)
         for jj in range(0, faces, 2):
             at = slice(jj * LANES, (jj + 2) * LANES)
-            found = dot(remote[...], twice(hot_remote[:, at]))
-            near[jj] = near[jj] + found[:, :LANES]
-            near[jj + 1] = near[jj + 1] + found[:, LANES:]
+            found = dot(both, twice(hot_remote[:, at]))
+            near[jj, rows, :] = near[jj, rows, :] + found[:, :LANES]
+            near[jj + 1, rows, :] = near[jj + 1, rows, :] + found[:, LANES:]
+
+    def near_update(ex):
+        for q in range(straight):
+            def pass_on(region, s, q=q):
+                arrival(ex, q, region, s).wait_recv()
+                forward(ex, q, region, s).start()
+
+            each_region(pass_on, core)
+        for q in range(count):
+            arrival(ex, q, 0, sibling).wait_recv()
+            if q == straight:
+                each_region(lambda region, s: arrival(ex, q, region, s).wait_recv(), core)
+            each_region(lambda region, s: arrival(ex, q, region, s).wait_recv(), 1 - core)
+            unpack(ex, q)
+            add_near(q)
+            starts = near_flux if q else None
+            if q < straight:
+                for chunk in chunks:
+                    for f, value in zip(chunk, flux_rows(1, near, chunk, parcels[q], starts)):
+                        near_flux[f] = value
         masks = [mask[o].astype(BF16) for o in range(3)]
         for chunk in chunks:
             pieces = []
-            for value in flux_rows(1, near, chunk):
+            for value in flux_rows(1, near, chunk, parcels[straight], near_flux):
                 hi, lo = split(value)
                 hi = [hi * masks[o] for o in range(3)]
                 lo = [lo * masks[o] for o in range(3)]
@@ -440,21 +474,23 @@
             add_out(chunk, dot(near_w[...], side_by_side(pieces)))
 
     def finish_sends(ex):
-        inner, lower, upper = exchange_copies(ex)
-        for copy in inner:
-            copy.wait_send()
-
-        @pl.when(has_low)
-        def _():
-            for copy in lower:
+        for q in range(count):
+            inner, lower, upper = exchange_copies(ex, q)
+            for copy in inner:
                 copy.wait_send()
 
-        @pl.when(has_high)
-        def _():
-            for copy in upper:
-                copy.wait_send()
-
-        each_region(lambda region, s: forward(ex, region, s).wait_send(), core)
+            @pl.when(has_low)
+            def _():
+                for copy in lower:
+                    copy.wait_send()
+
+            @pl.when(has_high)
+            def _():
+                for copy in upper:
+                    copy.wait_send()
+
+            if q < straight:
+                each_region(lambda region, s: forward(ex, q, region, s).wait_send(), core)
 
     def prepare_update():
         for j in range(faces):
@@ -542,13 +578,20 @@
     weight = lax.fori_loop(0, DEGREE // 2, two_orders, jnp.float32(1.0)) / (DEGREE + 1.0)
     loads[3].wait()
     proj_w[...] = columns3(by_face(proj_ref), depth)
+    ready = []
     for chunk in chunks:
         value = side_by_side(contract(y_even, fields, star_ref, chunk))
         taylor[DEGREE - 1, :, cols(chunk)] = value
         value = part[:, cols(chunk)] + weight * value
         part[:, cols(chunk)] = value
         project(chunk, value)
-    send_traces(0)
+        for q in ready:
+            start(0, q)
+        ready = [q for q, p in enumerate(parcels) if p[-1] == chunk[-1]]
+        for q in ready:
+            gather(0, q)
+    for q in ready:
+        start(0, q)
 
     for load in loads[4:]:
         load.wait()
@@ -556,8 +599,7 @@
     own_update()
     prepare_pairs()
     sum_slow()
-    take_arrivals(0)
-    near_update()
+    near_update(0)
     finish_sends(0)
 
     for chunk in pair_chunks:
@@ -584,7 +626,7 @@
 
     weight = lax.fori_loop(0, DEGREE // 2, two_pair_orders, jnp.float32(1.0)) / (DEGREE + 1.0)
     is_fast = lax.broadcasted_iota(jnp.int32, (modes, LANES), 1) < count_ref[0]
-    for chunk in pair_chunks:
+    for q, chunk in enumerate(pair_chunks):
         value = part_pair[:, cols(chunk)] + weight * contract_pairs(pair_even, chunk)
         for n, i in enumerate(chunk):
             item = value[:, lane(n)]
@@ -594,10 +636,12 @@
                 jnp.where(is_fast, both[q], slow[:, lane(f)]) for q, f in enumerate(mine)
             ]
             project(mine, side_by_side(mixed))
-    send_traces(1)
+        if q:
+            start(1, q - 1)
+        gather(1, q)
+    start(1, straight)
     own_update()
-    take_arrivals(1)
-    near_update()
+    near_update(1)
     finish_sends(1)
 
 
@@ -622,12 +666,14 @@
     slots = send_slots.shape[1]
     fold = LANES // slots
     face_pad, mode_pad = up(face_modes, 8), up(modes, 16)
-    table_rows = up((fields - 1) * face_modes + face_pad, 8 * fold)
     group = n_sub * slots
     width = fields * elems
     pairs = (fields + 1) // 2
     depth, rows3 = up(3 * modes, 16), up(3 * modes, 16)
     face_rows = 4 * face_pad
+    parcels = [min(4, fields - f) for f in range(0, fields, 4)]
+    rows_of = [up((p - 1) * face_modes + face_pad, 8 * fold) for p in parcels]
+    table_rows = sum(rows_of)
     any_space = pl.BlockSpec(memory_space=pl.ANY)
     vmem = pl.BlockSpec(memory_space=pltpu.VMEM)
     out = pl.pallas_call(
@@ -657,7 +703,8 @@
             pltpu.VMEM((4, table_rows, elems), F32),
             pltpu.VMEM((table_rows, 8 * elems), BF16),
             pltpu.VMEM((4, table_rows, elems), F32),
-            pltpu.VMEM((table_rows, 6 * group), BF16),
+            pltpu.VMEM((fields, face_rows, elems), F32),
+            pltpu.VMEM((table_rows, 3 * group), F32),
             pltpu.VMEM((rows3, depth), BF16),
             pltpu.VMEM((rows3, depth), BF16),
             pltpu.VMEM((face_rows, depth), BF16),
@@ -667,11 +714,9 @@
             pltpu.VMEM((3 * group, 4 * elems), BF16),
             pltpu.VMEM((4 * elems, 2 * LANES), BF16),
             pltpu.VMEM((3, face_rows, LANES), F32),
-            pltpu.VMEM((2, 2, table_rows // fold, LANES), F32),
-            pltpu.VMEM((2, 3, n_sub, table_rows // fold, LANES), F32),
-            pltpu.SemaphoreType.DMA((2, 3, n_sub)),
-            pltpu.SemaphoreType.DMA((2, 3, n_sub)),
-            pltpu.SemaphoreType.DMA((2, 3, n_sub)),
+            *[pltpu.SemaphoreType.DMA((2, len(parcels), 3, n_sub))] * 3,
+            *[pltpu.VMEM((2, 2, rows // fold, LANES), F32) for rows in rows_of],
+            *[pltpu.VMEM((2, 3, n_sub, rows // fold, LANES), F32) for rows in rows_of],
         ],
         compiler_params=pltpu.CompilerParams(collective_id=0, has_side_effects=True),
     )(

time: 26.2 us -> 28.6 us (1.092)
  the two profiles are of different devices: /device:TPU:21 before, /device:TPU:9 now
where the time goes in v2:
time: 28.6 us; the launch traced here: 28.4 us
  Pallas kernels  26.1 us (91%)
  local copies, waits for them, and re-layouts  1.66 us (6%)
  between operations  0.66 us (2%)
    pallas_call x1, Pallas kernels, local(): pl.pallas_call(functools.partial(kernel, (n_dom, n_sub, modes, fields, fa...  26.1 us
    unnamed x1, local copies, waits for them, and re-layouts  1.66 us

profile of v2, /device:TPU:9, one launch (start us, length us, event | category | flops | bytes accessed | tf_op | source)
XLA Modules:
  0.0 28.4 jit_solution(8876714768449429179)
XLA Ops:
  0.7 26.1 %shard_map.118 = f32[9,56,128]{2,1,0:T(8,128)} custom-call(f32[9,56,128]{2,1,0:T(8,128)} %bitcast.8, f32[9,9,3,128]{3,2,1,0:T(4,128)} %bitcast.9, f32[2,9,9,4,128]{4,3,2,1,0:T(4,128)} %bitcast.7, f32[3,56,56]{2,1,0:T(8,128)} %stiff_hbm.1, f32[3,56,56]{2,1,0:T(8,128)} %vol_hbm.1, f32[21,4,56]{2,1,0:T(4,128)} %bitcast.10, f32[21,4,56]{2,1,0:T(4,128)} %bitcast.11, ...), custom_call_target="tpu_custom_call" | custom-call | tf_op jit(solution)/shard_map/pallas_call | solution.py:679
  26.8 1.7 %copy.15 = f32[56,9,128]{2,0,1:T(8,128)} copy(f32[56,9,128]{2,0,1:T(8,128)} %bitcast.6) | data formatting | bytes 516096

commit v3 on v1

--- a/solution.py
+++ b/solution.py
@@ -526,24 +526,21 @@
         y_even[:, cols(chunk)] = stiff_rows(value)
     loads[2].wait()
 
-    def order(k, weight, source, target):
-        weight = weight / (k.astype(F32) + 2.0)
+    weight = 1.0
+    source, target = y_even, y_odd
+    for k in range(DEGREE - 1):
+        weight = weight / (k + 2)
         for chunk in chunks:
             value = side_by_side(contract(source, fields, star_ref, chunk))
             taylor[k, :, cols(chunk)] = value
             part[:, cols(chunk)] = part[:, cols(chunk)] + weight * value
             target[:, cols(chunk)] = stiff_rows(value)
-        return weight
-
-    def two_orders(k, weight):
-        weight = order(2 * k, weight, y_even, y_odd)
-        return order(2 * k + 1, weight, y_odd, y_even)
-
-    weight = lax.fori_loop(0, DEGREE // 2, two_orders, jnp.float32(1.0)) / (DEGREE + 1.0)
+        source, target = target, source
+    weight = weight / (DEGREE + 1)
     loads[3].wait()
     proj_w[...] = columns3(by_face(proj_ref), depth)
     for chunk in chunks:
-        value = side_by_side(contract(y_even, fields, star_ref, chunk))
+        value = side_by_side(contract(source, fields, star_ref, chunk))
         taylor[DEGREE - 1, :, cols(chunk)] = value
         value = part[:, cols(chunk)] + weight * value
         part[:, cols(chunk)] = value
@@ -570,22 +567,19 @@
         part_pair[:, cols(chunk)] = value
         pair_even[:, cols(chunk)] = stiff_rows(value)
 
-    def pair_order(k, weight, source, target):
-        weight = weight / (k.astype(F32) + 2.0)
+    weight = 1.0
+    source, target = pair_even, pair_odd
+    for k in range(DEGREE - 1):
+        weight = weight / (k + 2)
         for chunk in pair_chunks:
             value = contract_pairs(source, chunk)
             part_pair[:, cols(chunk)] = part_pair[:, cols(chunk)] + weight * value
             target[:, cols(chunk)] = stiff_rows(value)
-        return weight
-
-    def two_pair_orders(k, weight):
-        weight = pair_order(2 * k, weight, pair_even, pair_odd)
-        return pair_order(2 * k + 1, weight, pair_odd, pair_even)
-
-    weight = lax.fori_loop(0, DEGREE // 2, two_pair_orders, jnp.float32(1.0)) / (DEGREE + 1.0)
+        source, target = target, source
+    weight = weight / (DEGREE + 1)
     is_fast = lax.broadcasted_iota(jnp.int32, (modes, LANES), 1) < count_ref[0]
     for chunk in pair_chunks:
-        value = part_pair[:, cols(chunk)] + weight * contract_pairs(pair_even, chunk)
+        value = part_pair[:, cols(chunk)] + weight * contract_pairs(source, chunk)
         for n, i in enumerate(chunk):
             item = value[:, lane(n)]
             both = [item, pltpu.roll(item, half, 1)]
@@ -632,7 +626,7 @@
     vmem = pl.BlockSpec(memory_space=pltpu.VMEM)
     out = pl.pallas_call(
         functools.partial(kernel, (n_dom, n_sub, modes, fields, face_pad, slots)),
-        out_shape=jax.ShapeDtypeStruct((fields, modes, elems), F32),
+        out_shape=pltpu.VMEM((fields, modes, elems), F32),
         in_specs=[any_space] * 8 + [vmem] * 3 + [pl.BlockSpec(memory_space=pltpu.SMEM)],
         out_specs=vmem,
         scratch_shapes=[

time: 26.2 us -> 24.1 us (0.920)
  Pallas kernels: 23.7 us -> 22.6 us
  local copies, waits for them, and re-layouts: 1.66 us -> 0.7 us
    pallas_call x1, Pallas kernels: 23.7 us -> 22.6 us  [local(): pl.pallas_call(functools.partial(kernel, (n_dom, n_sub, modes, fields, fa...]
    unnamed x1, local copies, waits for them, and re-layouts: 1.66 us -> 0.7 us
where the time goes in v3:
time: 24.1 us; the launch traced here: 23.9 us
  Pallas kernels  22.6 us (94%)
  local copies, waits for them, and re-layouts  0.7 us (3%)
  between operations  0.66 us (3%)
    pallas_call x1, Pallas kernels, local(): pl.pallas_call(functools.partial(kernel, (n_dom, n_sub, modes, fields, fa...  22.6 us
    unnamed x1, local copies, waits for them, and re-layouts  0.7 us

profile of v3, /device:TPU:21, one launch (start us, length us, event | category | flops | bytes accessed | tf_op | source)
XLA Modules:
  0.0 23.9 jit_solution(15565200129989085302)
XLA Ops:
  0.7 22.6 %shard_map.118 = f32[9,56,128]{2,1,0:T(8,128)S(1)} custom-call(f32[9,56,128]{2,1,0:T(8,128)} %bitcast.8, f32[9,9,3,128]{3,2,1,0:T(4,128)} %bitcast.9, f32[2,9,9,4,128]{4,3,2,1,0:T(4,128)} %bitcast.7, f32[3,56,56]{2,1,0:T(8,128)} %stiff_hbm.1, f32[3,56,56]{2,1,0:T(8,128)} %vol_hbm.1, f32[21,4,56]{2,1,0:T(4,128)} %bitcast.10, f32[21,4,56]{2,1,0:T(4,128)} %bitcast.11, ...), custom_call_target="tpu_custom_call" | custom-call | tf_op jit(solution)/shard_map/pallas_call | solution.py:627
  23.2 0.7 %copy.14 = f32[56,9,128]{2,0,1:T(8,128)} copy(f32[56,9,128]{2,0,1:T(8,128)S(1)} %bitcast.6) | data formatting | bytes 516096

commit v4 on v3

--- a/solution.py
+++ b/solution.py
@@ -82,11 +82,14 @@
     proj_hbm,
     lift_hbm,
     maps_hbm,
+    near_idx_hbm,
+    orient_hbm,
+    slots_hbm,
+    count_ref,
+    out_ref,
     near_idx_ref,
     orient_ref,
     slots_ref,
-    count_ref,
-    out_ref,
     star_ref,
     flux_ref,
     stiff_ref,
@@ -141,6 +144,7 @@
         pltpu.make_async_copy(source, target, load_sem.at[i])
         for i, (source, target) in enumerate(
             [
+                (slots_hbm, slots_ref),
                 (stiff_hbm, stiff_ref),
                 (state_hbm, out_ref),
                 (star_hbm, star_ref),
@@ -149,6 +153,8 @@
                 (lift_hbm, lift_ref),
                 (maps_hbm, maps_ref),
                 (flux_hbm, flux_ref),
+                (near_idx_hbm, near_idx_ref),
+                (orient_hbm, orient_ref),
             ]
         )
     ]
@@ -194,6 +200,7 @@
         at = lax.broadcasted_iota(jnp.int32, (rows, LANES), 0)
         return jnp.where(at == row, 1.0, 0.0).astype(BF16)
 
+    loads[0].wait()
     tiled = dot(
         stacked(grow(slots_ref[...].astype(F32), 8)),
         at_columns(slots, LANES, lambda row, column: column % slots == row),
@@ -209,7 +216,7 @@
     def by_face(ref):
         return jnp.concatenate([grow(ref[:, j, :], face_pad) for j in range(faces)], axis=0)
 
-    loads[0].wait()
+    loads[1].wait()
     pred_w[...] = columns3(-by_direction(stiff_ref), depth)
 
     chunks = [tuple(range(f, min(f + 2, fields))) for f in range(0, fields, 2)]
@@ -274,9 +281,9 @@
                     j * face_pad : (j + 1) * face_pad, lane(i)
                 ]
 
-    def flux_rows(side, src, chunk):
+    def flux_rows(side, src, chunk, of=range(faces)):
         found = [[] for _ in chunk]
-        for j in range(faces):
+        for j in of:
             totals = [None] * len(chunk)
             for g in range(fields):
                 item = src[j, g * face_modes : g * face_modes + face_pad, :]
@@ -306,12 +313,11 @@
         for k in range(1, chips):
             target = {"dom": dom, "sub": 2 * lax.rem(chip + k, chips) + core}
             inner.append(out_copy(ex, 0, target, 0, k))
-        lower = [
-            out_copy(ex, 1, {"dom": dom - 1, "sub": 2 * c + core}, 2, c) for c in range(chips)
-        ]
-        upper = [
-            out_copy(ex, 1, {"dom": dom + 1, "sub": 2 * c + core}, 1, c) for c in range(chips)
-        ]
+        lower, upper = [], []
+        for k in reversed(range(chips)):
+            at = 2 * lax.rem(chip + k, chips) + core
+            lower.append(out_copy(ex, 1, {"dom": dom - 1, "sub": at}, 2, k))
+            upper.append(out_copy(ex, 1, {"dom": dom + 1, "sub": at}, 1, k))
         return inner, lower, upper
 
     def arrival(ex, region, s):
@@ -335,33 +341,35 @@
         )
 
     def each_region(do, side):
-        @pl.when(has_low)
-        def _():
-            for c in range(chips):
-                do(1, 2 * c + side)
-
-        @pl.when(has_high)
-        def _():
-            for c in range(chips):
-                do(2, 2 * c + side)
-
         for k in range(1, chips):
             do(0, 2 * lax.rem(chip + k, chips) + side)
+        for k in range(chips):
+            at = 2 * lax.rem(chip + k, chips) + side
+
+            @pl.when(has_low)
+            def _():
+                do(1, at)
+
+            @pl.when(has_high)
+            def _():
+                do(2, at)
 
     section = lax.broadcasted_iota(jnp.int32, (fold_rows, LANES), 1) // slots
 
     def send_traces(ex):
-        for j in range(faces):
-            hi, lo = split(trace[j])
-            table[:, lane(j)] = hi
-            table[:, lane(faces + j)] = lo
-        picked = dot(table[...], twice(hot_send[...]))
+        picked = []
+        for a in range(0, fold, 2):
+            rows = slice(a * fold_rows, (a + 2) * fold_rows)
+            for j in range(faces):
+                hi, lo = split(trace[j, rows, :])
+                table[rows, lane(j)] = hi
+                table[rows, lane(faces + j)] = lo
+            found = dot(table[rows, :], twice(hot_send[...]))
+            picked += [found[:fold_rows], found[fold_rows:]]
         for i in range(2):
-            packed = picked[:fold_rows, lane(i)]
+            packed = picked[0][:, lane(i)]
             for a in range(1, fold):
-                packed = jnp.where(
-                    section == a, picked[a * fold_rows : (a + 1) * fold_rows, lane(i)], packed
-                )
+                packed = jnp.where(section == a, picked[a][:, lane(i)], packed)
             send[ex, i] = packed
             if i == 0:
                 recv[ex, 0, sub] = packed
@@ -429,15 +437,17 @@
             found = dot(remote[...], twice(hot_remote[:, at]))
             near[jj] = near[jj] + found[:, :LANES]
             near[jj + 1] = near[jj + 1] + found[:, LANES:]
-        masks = [mask[o].astype(BF16) for o in range(3)]
-        for chunk in chunks:
-            pieces = []
-            for value in flux_rows(1, near, chunk):
-                hi, lo = split(value)
-                hi = [hi * masks[o] for o in range(3)]
-                lo = [lo * masks[o] for o in range(3)]
-                pieces.append(jnp.concatenate(hi + lo + hi, axis=0))
-            add_out(chunk, dot(near_w[...], side_by_side(pieces)))
+        for jj in range(0, faces, 2):
+            rows = slice(jj * face_pad, (jj + 2) * face_pad)
+            masks = [mask[o, rows, :].astype(BF16) for o in range(3)]
+            for chunk in chunks:
+                pieces = []
+                for value in flux_rows(1, near, chunk, (jj, jj + 1)):
+                    hi, lo = split(value)
+                    hi = [hi * masks[o] for o in range(3)]
+                    lo = [lo * masks[o] for o in range(3)]
+                    pieces.append(jnp.concatenate(hi + lo + hi, axis=0))
+                add_out(chunk, dot(near_w[jj // 2], side_by_side(pieces)))
 
     def finish_sends(ex):
         inner, lower, upper = exchange_copies(ex)
@@ -477,27 +487,30 @@
         own_w[:, :face_rows] = hi
         own_w[:, face_rows : 2 * face_rows] = hi
         own_w[:, 2 * face_rows :] = lo
-        turned = None
         map_pad = up(face_pad, 16)
-        for o in range(3):
-            place = at_columns(
-                face_modes,
-                3 * face_rows,
-                lambda row, column: (column // face_rows == o) & (column % face_pad == row),
-            )
-            both = dot(stacked(grow(maps_ref[o], map_pad)), place)
-            term = both[:face_pad] + both[map_pad : map_pad + face_pad]
-            turned = term if turned is None else turned + term
-        turned = jnp.concatenate([turned] * faces, axis=0)
-        row = lax.broadcasted_iota(jnp.int32, turned.shape, 0)
-        column = lax.broadcasted_iota(jnp.int32, turned.shape, 1)
-        turned = jnp.where(column % face_rows // face_pad == row // face_pad, turned, 0.0)
-        turned_hi, turned_lo = split(turned)
-        value = dot(hi, turned_hi) + dot(lo, turned_hi) + dot(hi, turned_lo)
-        hi, lo = split(value)
-        near_w[:, : 3 * face_rows] = hi
-        near_w[:, 3 * face_rows : 6 * face_rows] = hi
-        near_w[:, 6 * face_rows :] = lo
+        pair_rows = 2 * face_pad
+        maps = [stacked(grow(maps_ref[o], map_pad)) for o in range(3)]
+        for jj in range(0, faces, 2):
+            turned = None
+            for o in range(3):
+                place = at_columns(
+                    face_modes,
+                    3 * pair_rows,
+                    lambda row, column: (column // pair_rows == o) & (column % face_pad == row),
+                )
+                both = dot(maps[o], place)
+                term = both[:face_pad] + both[map_pad : map_pad + face_pad]
+                turned = term if turned is None else turned + term
+            turned = jnp.concatenate([turned] * faces, axis=0)
+            row = lax.broadcasted_iota(jnp.int32, turned.shape, 0)
+            column = lax.broadcasted_iota(jnp.int32, turned.shape, 1)
+            same_face = column % pair_rows // face_pad + jj == row // face_pad
+            turned_hi, turned_lo = split(jnp.where(same_face, turned, 0.0))
+            value = dot(hi, turned_hi) + dot(lo, turned_hi) + dot(hi, turned_lo)
+            value_hi, value_lo = split(value)
+            near_w[jj // 2, :, : 3 * pair_rows] = value_hi
+            near_w[jj // 2, :, 3 * pair_rows : 6 * pair_rows] = value_hi
+            near_w[jj // 2, :, 6 * pair_rows :] = value_lo
 
     def prepare_pairs():
         low = lax.broadcasted_iota(jnp.int32, (8, LANES), 1) < half
@@ -519,12 +532,12 @@
                 total = total + ((2.0 ** (k + 2) - 2.0) * weight) * taylor[k, :, lane(f)]
             slow[:, lane(f)] = total
 
-    loads[1].wait()
+    loads[2].wait()
     for chunk in chunks:
         value = side_by_side([out_ref[f] for f in chunk])
         part[:, cols(chunk)] = value
         y_even[:, cols(chunk)] = stiff_rows(value)
-    loads[2].wait()
+    loads[3].wait()
 
     weight = 1.0
     source, target = y_even, y_odd
@@ -537,7 +550,7 @@
             target[:, cols(chunk)] = stiff_rows(value)
         source, target = target, source
     weight = weight / (DEGREE + 1)
-    loads[3].wait()
+    loads[4].wait()
     proj_w[...] = columns3(by_face(proj_ref), depth)
     for chunk in chunks:
         value = side_by_side(contract(source, fields, star_ref, chunk))
@@ -547,7 +560,7 @@
         project(chunk, value)
     send_traces(0)
 
-    for load in loads[4:]:
+    for load in loads[5:]:
         load.wait()
     prepare_update()
     own_update()
@@ -627,9 +640,12 @@
     out = pl.pallas_call(
         functools.partial(kernel, (n_dom, n_sub, modes, fields, face_pad, slots)),
         out_shape=pltpu.VMEM((fields, modes, elems), F32),
-        in_specs=[any_space] * 8 + [vmem] * 3 + [pl.BlockSpec(memory_space=pltpu.SMEM)],
+        in_specs=[any_space] * 11 + [pl.BlockSpec(memory_space=pltpu.SMEM)],
         out_specs=vmem,
         scratch_shapes=[
+            pltpu.VMEM(neighbours.shape, jnp.int32),
+            pltpu.VMEM(face_orient.shape, jnp.int32),
+            pltpu.VMEM(send_slots.shape, jnp.int32),
             pltpu.VMEM((fields, fields, 3, elems), F32),
             pltpu.VMEM((2, fields, fields, 4, elems), F32),
             pltpu.VMEM((3, modes, modes), F32),
@@ -637,7 +653,7 @@
             pltpu.VMEM((face_modes, 4, modes), F32),
             pltpu.VMEM((face_modes, 4, modes), F32),
             pltpu.VMEM((3, face_modes, face_modes), F32),
-            pltpu.SemaphoreType.DMA((8,)),
+            pltpu.SemaphoreType.DMA((11,)),
             pltpu.VMEM((fields, pairs, 3, elems), F32),
             pltpu.VMEM((3 * modes, width), F32),
             pltpu.VMEM((3 * modes, width), F32),
@@ -656,7 +672,7 @@
             pltpu.VMEM((rows3, depth), BF16),
             pltpu.VMEM((face_rows, depth), BF16),
             pltpu.VMEM((mode_pad, 3 * face_rows), BF16),
-            pltpu.VMEM((mode_pad, 9 * face_rows), BF16),
+            pltpu.VMEM((2, mode_pad, 9 * face_rows // 2), BF16),
             pltpu.VMEM((4 * elems, 4 * elems), BF16),
             pltpu.VMEM((3 * group, 4 * elems), BF16),
             pltpu.VMEM((4 * elems, 2 * LANES), BF16),

time: 24.1 us -> 23.1 us (0.959)
  Pallas kernels: 22.6 us -> 21.6 us
    pallas_call x1, Pallas kernels: 22.6 us -> 21.6 us  [local(): pl.pallas_call(functools.partial(kernel, (n_dom, n_sub, modes, fields, fa...]
where the time goes in v4:
time: 23.1 us; the launch traced here: 23 us
  Pallas kernels  21.6 us (94%)
  local copies, waits for them, and re-layouts  0.7 us (3%)
  between operations  0.66 us (3%)
    pallas_call x1, Pallas kernels, local(): pl.pallas_call(functools.partial(kernel, (n_dom, n_sub, modes, fields, fa...  21.6 us
    unnamed x1, local copies, waits for them, and re-layouts  0.7 us

profile of v4, /device:TPU:21, one launch (start us, length us, event | category | flops | bytes accessed | tf_op | source)
XLA Modules:
  0.0 23.0 jit_solution(13120552117822034985)
XLA Ops:
  0.7 21.6 %shard_map.118 = f32[9,56,128]{2,1,0:T(8,128)S(1)} custom-call(f32[9,56,128]{2,1,0:T(8,128)} %bitcast.8, f32[9,9,3,128]{3,2,1,0:T(4,128)} %bitcast.9, f32[2,9,9,4,128]{4,3,2,1,0:T(4,128)} %bitcast.7, f32[3,56,56]{2,1,0:T(8,128)} %stiff_hbm.1, f32[3,56,56]{2,1,0:T(8,128)} %vol_hbm.1, f32[21,4,56]{2,1,0:T(4,128)} %bitcast.10, f32[21,4,56]{2,1,0:T(4,128)} %bitcast.11, ...), custom_call_target="tpu_custom_call" | custom-call | tf_op jit(solution)/shard_map/pallas_call | solution.py:640
  22.3 0.7 %copy.14 = f32[56,9,128]{2,0,1:T(8,128)} copy(f32[56,9,128]{2,0,1:T(8,128)S(1)} %bitcast.6) | data formatting | bytes 516096

commit v5 on v4

--- a/solution.py
+++ b/solution.py
@@ -234,22 +234,21 @@
     def stiff_rows(value):
         return dot(pred_w[...], rows3(value, depth))[: 3 * modes]
 
-    blocks = [(start, min(16, modes - start)) for start in range(0, modes, 16)]
-
-    def contract(source, terms, rows, targets):
+    def contract(source, terms, rows, targets, size, sums):
         values = [[] for _ in targets]
-        for start, count in blocks:
-            totals = [[None] * 3 for _ in targets]
+        for start in range(0, modes, size):
+            count = min(size, modes - start)
+            totals = [[None] * sums for _ in targets]
             for g in range(terms):
                 for d in range(3):
                     first = d * modes + start
                     item = source[first : first + count, lane(g)]
                     for i, f in enumerate(targets):
                         term = row_of(rows, f, g, d) * item
-                        total = totals[i][d]
-                        totals[i][d] = term if total is None else total + term
+                        total = totals[i][d % sums]
+                        totals[i][d % sums] = term if total is None else total + term
             for i, total in enumerate(totals):
-                values[i].append(total[0] + total[1] + total[2])
+                values[i].append(functools.reduce(jnp.add, total))
         return [jnp.concatenate(value, axis=0) for value in values]
 
     low_half = lax.broadcasted_iota(jnp.int32, (modes, LANES), 1) < half
@@ -259,7 +258,7 @@
 
     def contract_pairs(source, chunk):
         targets = [f for i in chunk for f in (2 * i, 2 * i + 1) if f < fields]
-        values = contract(source, pairs, star_pair, targets)
+        values = contract(source, pairs, star_pair, targets, 56, 1)
         if len(targets) < 2 * len(chunk):
             values.append(jnp.zeros((modes, LANES), F32))
         result = []
@@ -302,7 +301,7 @@
         return pltpu.make_async_remote_copy(
             src_ref=send.at[ex, which],
             dst_ref=recv.at[ex, region, sub],
-            send_sem=send_sem.at[ex, region, at],
+            send_sem=send_sem.at[region, at],
             recv_sem=recv_sem.at[ex, region, sub],
             device_id=target,
             device_id_type=pl.DeviceIdType.MESH,
@@ -324,7 +323,7 @@
         return pltpu.make_async_remote_copy(
             src_ref=send.at[ex, 0],
             dst_ref=recv.at[ex, region, s],
-            send_sem=send_sem.at[ex, region, 0],
+            send_sem=send_sem.at[region, 0],
             recv_sem=recv_sem.at[ex, region, s],
             device_id={"dom": dom, "sub": sub},
             device_id_type=pl.DeviceIdType.MESH,
@@ -334,7 +333,7 @@
         return pltpu.make_async_remote_copy(
             src_ref=recv.at[ex, region, s],
             dst_ref=recv.at[ex, region, s],
-            send_sem=forward_sem.at[ex, region, s],
+            send_sem=forward_sem.at[region, s // 2],
             recv_sem=recv_sem.at[ex, region, s],
             device_id={"dom": dom, "sub": sibling},
             device_id_type=pl.DeviceIdType.MESH,
@@ -401,7 +400,7 @@
         for chunk in chunks:
             y_even[:, cols(chunk)] = dot(vol_w[...], part_rows[:, cols(chunk)])[: 3 * modes]
         for chunk in chunks:
-            volume = side_by_side(contract(y_even, fields, star_ref, chunk))
+            volume = side_by_side(contract(y_even, fields, star_ref, chunk, 16, 3))
             own = side_by_side(flux_rows(0, trace, chunk))
             add_out(chunk, volume + dot(own_w[...], rows3(own, 3 * face_rows))[:modes])
 
@@ -417,13 +416,18 @@
         for region in range(3):
             for b in range(n_sub // fold):
                 parts = [recv[ex, region, b * fold + i] for i in range(fold)]
+                turned = []
+                for shift in range(fold):
+                    value = parts[shift]
+                    for a in range(1, fold):
+                        value = jnp.where(section == a, parts[(a + shift) % fold], value)
+                    if shift:
+                        value = pltpu.roll(value, shift * slots, 1)
+                    turned.append(value)
                 for a in range(fold):
-                    value = None
-                    for i in range(fold):
-                        moved = parts[i]
-                        if i != a:
-                            moved = pltpu.roll(moved, ((i - a) * slots) % LANES, 1)
-                        value = moved if value is None else jnp.where(section == i, moved, value)
+                    value = turned[-a % fold]
+                    for i in range(1, fold):
+                        value = jnp.where(section == i, turned[(i - a) % fold], value)
                     first = region * group + b * LANES
                     rows = slice(a * fold_rows, (a + 1) * fold_rows)
                     hi, lo = split(value)
@@ -538,22 +542,22 @@
         part[:, cols(chunk)] = value
         y_even[:, cols(chunk)] = stiff_rows(value)
     loads[3].wait()
+    loads[4].wait()
+    proj_w[...] = columns3(by_face(proj_ref), depth)
 
     weight = 1.0
     source, target = y_even, y_odd
     for k in range(DEGREE - 1):
         weight = weight / (k + 2)
         for chunk in chunks:
-            value = side_by_side(contract(source, fields, star_ref, chunk))
+            value = side_by_side(contract(source, fields, star_ref, chunk, 16, 3))
             taylor[k, :, cols(chunk)] = value
             part[:, cols(chunk)] = part[:, cols(chunk)] + weight * value
             target[:, cols(chunk)] = stiff_rows(value)
         source, target = target, source
     weight = weight / (DEGREE + 1)
-    loads[4].wait()
-    proj_w[...] = columns3(by_face(proj_ref), depth)
     for chunk in chunks:
-        value = side_by_side(contract(source, fields, star_ref, chunk))
+        value = side_by_side(contract(source, fields, star_ref, chunk, 16, 3))
         taylor[DEGREE - 1, :, cols(chunk)] = value
         value = part[:, cols(chunk)] + weight * value
         part[:, cols(chunk)] = value
@@ -679,9 +683,9 @@
             pltpu.VMEM((3, face_rows, LANES), F32),
             pltpu.VMEM((2, 2, table_rows // fold, LANES), F32),
             pltpu.VMEM((2, 3, n_sub, table_rows // fold, LANES), F32),
+            pltpu.SemaphoreType.DMA((3, n_sub // 2)),
             pltpu.SemaphoreType.DMA((2, 3, n_sub)),
-            pltpu.SemaphoreType.DMA((2, 3, n_sub)),
-            pltpu.SemaphoreType.DMA((2, 3, n_sub)),
+            pltpu.SemaphoreType.DMA((3, n_sub // 2)),
         ],
         compiler_params=pltpu.CompilerParams(collective_id=0, has_side_effects=True),
     )(

time: 23.1 us -> 22.7 us (0.983)
  Pallas kernels: 21.6 us -> 21.2 us
    pallas_call x1, Pallas kernels: 21.6 us -> 21.2 us  [local(): pl.pallas_call(functools.partial(kernel, (n_dom, n_sub, modes, fields, fa...]
where the time goes in v5:
time: 22.7 us; the launch traced here: 22.5 us
  Pallas kernels  21.2 us (93%)
  local copies, waits for them, and re-layouts  0.7 us (3%)
  between operations  0.66 us (3%)
    pallas_call x1, Pallas kernels, local(): pl.pallas_call(functools.partial(kernel, (n_dom, n_sub, modes, fields, fa...  21.2 us
    unnamed x1, local copies, waits for them, and re-layouts  0.7 us

profile of v5, /device:TPU:21, one launch (start us, length us, event | category | flops | bytes accessed | tf_op | source)
XLA Modules:
  0.0 22.5 jit_solution(12706145928790938194)
XLA Ops:
  0.7 21.2 %shard_map.118 = f32[9,56,128]{2,1,0:T(8,128)S(1)} custom-call(f32[9,56,128]{2,1,0:T(8,128)} %bitcast.8, f32[9,9,3,128]{3,2,1,0:T(4,128)} %bitcast.9, f32[2,9,9,4,128]{4,3,2,1,0:T(4,128)} %bitcast.7, f32[3,56,56]{2,1,0:T(8,128)} %stiff_hbm.1, f32[3,56,56]{2,1,0:T(8,128)} %vol_hbm.1, f32[21,4,56]{2,1,0:T(4,128)} %bitcast.10, f32[21,4,56]{2,1,0:T(4,128)} %bitcast.11, ...), custom_call_target="tpu_custom_call" | custom-call | tf_op jit(solution)/shard_map/pallas_call | solution.py:644
  21.8 0.7 %copy.14 = f32[56,9,128]{2,0,1:T(8,128)} copy(f32[56,9,128]{2,0,1:T(8,128)S(1)} %bitcast.6) | data formatting | bytes 516096
